TPU v7x, 512 devices: a whole 4x4x16 slice. The times are simulated.
512 devices in a mesh: fx: 8 (over y_lo, x), fy: 16 (over z), fz: 4 (over y_hi, core).
Axes of the slice: x: 4, y: 4 (y_hi: 2, y_lo: 2; y = y_hi * 2 + y_lo), z: 16, core: 2. Of those that a mesh axis runs over, the one named last changes fastest.
Arguments:
- density: float32 [64, 128, 512], P('fx', 'fy', 'fz'), may hold values from 0.8 to 1.25
- velocity: float32 [3, 64, 128, 512], P(None, 'fx', 'fy', 'fz'), may hold values from -2 to 2
- pressure: float32 [64, 128, 512], P('fx', 'fy', 'fz'), may hold values from 0.7 to 1.4
- acoustic: float32 [8192, 4, 512], P(('fx', 'fy', 'fz')), may hold values from -6 to 6
- sound_speed: float32 [8192], P(('fx', 'fy', 'fz')), may hold values from 0.5 to 2
- derivative: float32 [8, 8], replicated, may hold values from -2 to 2
- mode_basis: float32 [8, 8], replicated, may hold values from -2 to 2
- neighbours: int32 [8192, 6], P(('fx', 'fy', 'fz')), may hold values from 0 to 8191, as said below
- block_owner: int32 [8, 16, 4, 16, 1], P('fx', 'fy', 'fz'), may hold values from 0 to 15; in each aligned block of 16 rows (0 to 15, 16 to 31, ..., all dimensions but the last counted through in order) at most 2 rows name the same one
- block_element: int32 [8, 16, 4, 16], P('fx', 'fy', 'fz'), may hold values from 0 to 15
Outputs:
- flow_state: float32 [5, 64, 128, 512], P(None, 'fx', 'fy', 'fz')
- sound_state: float32 [8192, 4, 512], P(('fx', 'fy', 'fz'))
Inputs may be any that keep to these rules, and one draw needn't show every extreme that they name: `neighbours`: across faces -x, -y, -z the neighbour of element e lies in e - 16 to e, across faces +x, +y, +z in e to e + 16. `block_owner`: the 16 blocks of one flow device name one fy index at most 2 times.
All inputs are finite; a program needn't handle non-finite values.
Results may differ from a plain program's by a relative error of at most 0.0001.
Values sent between devices are 32-bit elements; how exact they have to be, the bound alone decides.
A program may use at most 64 MiB of HBM per device.

v0:
```python
import jax
import jax.numpy as jnp
from jax import lax
from jax.sharding import PartitionSpec as P

HEAT_RATIO = 1.4
TIME_STEP = 0.1
VISCOSITY = 0.05
PENALTY = 0.5
HIGHEST = lax.Precision.HIGHEST


def padded_2(cells, sides, width, closed):
    for axis, dim in sides:
        count = lax.axis_size(axis)
        ends = count if closed else count - 1
        head = lax.slice_in_dim(cells, 0, width, axis=dim)
        tail = lax.slice_in_dim(cells, cells.shape[dim] - width, cells.shape[dim], axis=dim)
        cells = jnp.concatenate(
            [
                lax.ppermute(tail, axis, [(i, (i + 1) % count) for i in range(ends)]),
                cells,
                lax.ppermute(head, axis, [((i + 1) % count, i) for i in range(ends)]),
            ],
            axis=dim,
        )
    return cells


def cut_range(values, along, start_at, stop_at):
    return lax.slice_in_dim(values, start_at, stop_at, axis=along + 1)


def interior(padded, along):
    for other in range(3):
        if other != along:
            padded = cut_range(padded, other, 1, padded.shape[other + 1] - 1)
    return padded


def flow_section(padded):
    center = padded[:, 1:-1, 1:-1, 1:-1]
    velocity_mid = center[1:4] / center[0]
    flow_rate = jnp.zeros_like(center)
    laplace = jnp.zeros_like(velocity_mid)
    slopes = []
    for along in range(3):
        stripe = interior(padded, along)
        length = stripe.shape[along + 1]
        velocity_cells = stripe[1:4] / stripe[0]
        pressure_cells = (HEAT_RATIO - 1.0) * (
            stripe[4] - 0.5 * jnp.sum(stripe[1:4] * velocity_cells, 0)
        )
        signal_speed = (
            jnp.abs(velocity_cells[along])
            + jnp.sqrt(HEAT_RATIO * jnp.abs(pressure_cells) / stripe[0])
        )[None]
        unit_axis = (jnp.arange(3) == along).astype(jnp.float32)
        momentum_flux = (
            stripe[1:4] * velocity_cells[along] + unit_axis[:, None, None, None] * pressure_cells
        )
        fluxes = jnp.concatenate(
            [
                stripe[1 + along][None],
                momentum_flux,
                ((stripe[4] + pressure_cells) * velocity_cells[along])[None],
            ],
            0,
        )
        wave_speed = jnp.maximum(
            cut_range(signal_speed, along, 0, length - 1), cut_range(signal_speed, along, 1, length)
        )
        face_flux = 0.5 * (
            cut_range(fluxes, along, 0, length - 1) + cut_range(fluxes, along, 1, length)
        ) - 0.5 * wave_speed * (
            cut_range(stripe, along, 1, length) - cut_range(stripe, along, 0, length - 1)
        )
        flow_rate = flow_rate - (
            cut_range(face_flux, along, 1, length - 1) - cut_range(face_flux, along, 0, length - 2)
        )
        laplace = (
            laplace
            + cut_range(stripe[1:4], along, 2, length)
            + cut_range(stripe[1:4], along, 0, length - 2)
            - 2.0 * center[1:4]
        )
        slopes.append(
            0.5
            * (
                cut_range(velocity_cells, along, 2, length)
                - cut_range(velocity_cells, along, 0, length - 2)
            )
        )
    empty_row = jnp.zeros_like(center[:1])
    flow_rate = flow_rate + VISCOSITY * jnp.concatenate([empty_row, laplace, empty_row], 0)
    vorticity = jnp.stack(
        [slopes[1][2] - slopes[2][1], slopes[2][0] - slopes[0][2], slopes[0][1] - slopes[1][0]]
    )
    lamb_vector = jnp.stack(
        [
            vorticity[1] * velocity_mid[2] - vorticity[2] * velocity_mid[1],
            vorticity[2] * velocity_mid[0] - vorticity[0] * velocity_mid[2],
            vorticity[0] * velocity_mid[1] - vorticity[1] * velocity_mid[0],
        ]
    )
    return (flow_rate, lamb_vector)


def conserved(density, velocity, pressure):
    energy = pressure / (HEAT_RATIO - 1.0) + 0.5 * density * jnp.sum(velocity * velocity, 0)
    return jnp.concatenate([density[None], density[None] * velocity, energy[None]], 0)


def apply_cube(fields, first_matrix, inner_table):
    row_count = fields.shape[0]
    cube = fields.reshape(row_count, 8, 64)
    along_first = jnp.einsum("xa,rab->rxb", first_matrix, cube, precision=HIGHEST).reshape(
        row_count * 8, 64
    )
    return jnp.dot(along_first, inner_table, precision=HIGHEST).reshape(row_count, 512)


def nodal_slopes(fields, derivative):
    row_count = fields.shape[0]
    identity = jnp.eye(8, dtype=jnp.float32)
    slope_y_table = jnp.kron(derivative.T, identity)
    slope_z_table = jnp.kron(identity, derivative.T)
    cube = fields.reshape(row_count, 8, 64)
    slope_x = jnp.einsum("xa,rab->rxb", derivative, cube, precision=HIGHEST).reshape(row_count, 512)
    flat = fields.reshape(row_count * 8, 64)
    slope_y = jnp.dot(flat, slope_y_table, precision=HIGHEST).reshape(row_count, 512)
    slope_z = jnp.dot(flat, slope_z_table, precision=HIGHEST).reshape(row_count, 512)
    return (slope_x, slope_y, slope_z)


def extract(state_now):
    element_count = state_now.shape[0]
    cube = state_now.reshape(element_count, 4, 8, 8, 8)
    surfaces = [
        cube[:, :, 0],
        cube[:, :, 7],
        cube[:, :, :, 0],
        cube[:, :, :, 7],
        cube[:, :, :, :, 0],
        cube[:, :, :, :, 7],
    ]
    return jnp.concatenate([surface.reshape(element_count, 4, 64) for surface in surfaces], 2)


def lift_faces(jumps):
    element_count = jumps.shape[0]
    faces = jumps.reshape(element_count, 4, 6, 8, 8)
    gap_x = jnp.zeros((element_count, 4, 6, 8, 8), jnp.float32)
    gap_y = jnp.zeros((element_count, 4, 8, 6, 8), jnp.float32)
    gap_z = jnp.zeros((element_count, 4, 8, 8, 6), jnp.float32)
    lifted_x = jnp.concatenate([faces[:, :, 0][:, :, None], gap_x, faces[:, :, 1][:, :, None]], 2)
    lifted_y = jnp.concatenate(
        [faces[:, :, 2][:, :, :, None], gap_y, faces[:, :, 3][:, :, :, None]], 3
    )
    lifted_z = jnp.concatenate([faces[:, :, 4][..., None], gap_z, faces[:, :, 5][..., None]], 4)
    return (lifted_x + lifted_y + lifted_z).reshape(element_count, 4, 512)


def face_jumps(own_faces, face_table, neighbour_rows):
    pieces = []
    for facet_index in range(6):
        opposite = facet_index ^ 1
        remote = face_table[:, :, opposite * 64 : (opposite + 1) * 64][
            neighbour_rows[:, facet_index]
        ]
        pieces.append(remote - own_faces[:, :, facet_index * 64 : (facet_index + 1) * 64])
    return jnp.concatenate(pieces, 2)


def acoustic_rate(state_now, jumps, source, sound_speed, derivative):
    element_count = state_now.shape[0]
    slope_x, slope_y, slope_z = nodal_slopes(state_now.reshape(element_count * 4, 512), derivative)
    slope_x = slope_x.reshape(element_count, 4, 512)
    slope_y = slope_y.reshape(element_count, 4, 512)
    slope_z = slope_z.reshape(element_count, 4, 512)
    pressure_gradient = jnp.stack([slope_x[:, 0], slope_y[:, 0], slope_z[:, 0]], 1)
    divergence = slope_x[:, 1] + slope_y[:, 2] + slope_z[:, 3]
    lifted = lift_faces(jumps)
    rate_pressure = -(sound_speed * sound_speed)[:, None] * divergence + PENALTY * lifted[:, 0]
    rate_velocity = -pressure_gradient + source + PENALTY * lifted[:, 1:4]
    return jnp.concatenate([rate_pressure[:, None], rate_velocity], 1)


def project_local(lamb_vector, mode_basis, pair_table):
    cells_x, cells_y, cells_z = (lamb_vector.shape[1], lamb_vector.shape[2], lamb_vector.shape[3])
    blocks = lamb_vector.reshape(3, cells_x // 8, 8, cells_y // 8, 8, cells_z // 8, 8)
    blocks = blocks.transpose(1, 3, 5, 0, 2, 4, 6).reshape(-1, 512)
    return apply_cube(blocks, mode_basis, pair_table).reshape(-1, 1536)


def route(projected, owners, elements_of, element_count):
    peers = lax.axis_size("fy")
    blocks_here = owners.shape[0]
    capacity = max(2, 2 * blocks_here // peers)
    matches = (owners[:, None] == jnp.arange(peers, dtype=jnp.int32)[None, :]).astype(jnp.int32)
    position = jnp.sum((jnp.cumsum(matches, 0) - 1) * matches, 1)
    slot_index = owners * capacity + position
    chooser = jnp.arange(peers * capacity, dtype=jnp.int32)[:, None] == slot_index[None, :]
    packed = jnp.dot(chooser.astype(jnp.float32), projected, precision=HIGHEST).reshape(
        peers, capacity, 1536
    )
    labels = (jnp.sum(jnp.where(chooser, elements_of[None, :] + 1, 0), 1) - 1).reshape(
        peers, capacity
    )
    arrived, arrived_labels = (
        lax.all_to_all(packed, "fy", split_axis=0, concat_axis=0, tiled=True),
        lax.all_to_all(labels, "fy", split_axis=0, concat_axis=0, tiled=True),
    )
    placer = (
        jnp.arange(element_count, dtype=jnp.int32)[:, None] == arrived_labels.reshape(-1)[None, :]
    ).astype(jnp.float32)
    summed = jnp.dot(placer, arrived.reshape(peers * capacity, 1536), precision=HIGHEST)
    return summed.reshape(element_count, 3, 512)


def per_device(
    density,
    velocity,
    pressure,
    acoustic,
    sound_speed,
    derivative,
    mode_basis,
    neighbours,
    block_owner,
    block_element,
):
    pair_table = jnp.kron(mode_basis, mode_basis).T
    element_count = acoustic.shape[0]
    device = lax.axis_index(("fx", "fy", "fz"))
    neighbour_rows = neighbours - (device - 1) * element_count
    owners = block_owner.reshape(-1)
    elements_of = block_element.reshape(-1)

    def section(flow_now, sound_now):
        padded = padded_2(flow_now, (("fx", 1), ("fy", 2), ("fz", 3)), 1, True)
        flow_rate, lamb_vector = flow_section(padded)
        source = route(
            project_local(lamb_vector, mode_basis, pair_table), owners, elements_of, element_count
        )
        wide_state = padded_2(sound_now, ((("fx", "fy", "fz"), 0),), element_count, False)
        face_table = extract(wide_state)
        own_faces = face_table[element_count : 2 * element_count]
        jumps = face_jumps(own_faces, face_table, neighbour_rows)
        return (flow_rate, acoustic_rate(sound_now, jumps, source, sound_speed, derivative))

    flow_start = conserved(density, velocity, pressure)
    rate_one, sound_rate = section(flow_start, acoustic)
    flow_one = flow_start + TIME_STEP * rate_one
    sound_one = acoustic + TIME_STEP * sound_rate
    rate_two, sound_rate = section(flow_one, sound_one)
    flow_two = 0.75 * flow_start + 0.25 * (flow_one + TIME_STEP * rate_two)
    sound_two = 0.75 * acoustic + 0.25 * (sound_one + TIME_STEP * sound_rate)
    rate_three, sound_rate = section(flow_two, sound_two)
    flow_state = 1.0 / 3.0 * flow_start + 2.0 / 3.0 * (flow_two + TIME_STEP * rate_three)
    sound_state = 1.0 / 3.0 * acoustic + 2.0 / 3.0 * (sound_two + TIME_STEP * sound_rate)
    return (flow_state, sound_state)


def solution(mesh):
    placed = (
        P("fx", "fy", "fz"),
        P(None, "fx", "fy", "fz"),
        P("fx", "fy", "fz"),
        P(("fx", "fy", "fz"), None, None),
        P(("fx", "fy", "fz")),
        P(),
        P(),
        P(("fx", "fy", "fz"), None),
        P("fx", "fy", "fz", None, None),
        P("fx", "fy", "fz", None),
    )
    return jax.shard_map(
        per_device,
        mesh=mesh,
        in_specs=placed,
        out_specs=(P(None, "fx", "fy", "fz"), P(("fx", "fy", "fz"), None, None)),
        check_vma=False,
    )
```

profile of v0, /device:TPU:2, one launch (start us, length us, event | category | flops | bytes accessed | tf_op | source)
XLA Modules:
  0.0 274.9 jit_solution(14640166213196326447)
XLA Ops:
  0.7 1.7 copy.259
  2.3 13.4 %collective-permute-start.19 = (f32[16,4,512]{2,0,1:T(8,128)}, f32[16,4,512]{2,0,1:T(8,128)}, u32[]{:S(2)}, u32[]{:S(2)}) collective-permute-start(f32[16,4,512]{2,0,1:T(8,128)} %copy.259), channel_id=1, source_target_pairs={{1,0},{2,1},{3,2},{4,3},{5,4},{6,5},{7,6},{8,7},{9,8},{10,9},{11,1... | collective-permute-start | bytes 393224 | tf_op jit(solution)/shard_map/ppermute | solution.py:23
  15.8 1.9 collective-permute-start.18
  17.7 0.9 broadcast_divide_fusion.2
  18.6 0.8 add_bitcast_fusion
  19.4 0.8 pad_maximum_fusion.31
  20.2 1.9 collective-permute-start.1
  22.1 3.9 %collective-permute-start = (f32[5,1,8,128]{3,2,1,0:T(8,128)S(1)}, f32[5,1,8,128]{3,2,1,0:T(8,128)S(1)}, u32[]{:S(2)}, u32[]{:S(2)}) collective-permute-start(f32[5,1,8,128]{3,2,1,0:T(8,128)S(1)} %get-tuple-element.132), channel_id=1, source_target_pairs={{0,64},{64,128},{128,192},{192,256},{256,320},{320,384},{384,448},... | collective-permute-start | bytes 61448 | tf_op jit(solution)/shard_map/ppermute | solution.py:21
  26.1 0.7 fusion.181
  26.8 0.8 select_reduce_fusion.1
  29.8 6.3 %all-to-all-start = ((s32[16,1,2]{2,1,0:T(1,128)}), s32[16,1,2]{2,1,0:T(1,128)S(1)}, u32[]{:S(2)}, u32[]{:S(2)}) async-start(s32[16,1,2]{2,1,0:T(1,128)} %bitcast.80), calls=%async_computation | async-start | bytes 16384 | tf_op jit(solution)/shard_map/all_to_all | solution.py:212
  36.2 1.0 reshape_reshape.65
  41.1 0.7 fusion.221
  44.0 0.7 mul.1278
  46.6 1.8 all-to-all-done
  50.3 3.2 %collective-permute-start.3 = (f32[5,10,1,128]{3,2,1,0:T(1,128)S(1)}, f32[5,10,1,128]{3,2,1,0:T(1,128)S(1)}, u32[]{:S(2)}, u32[]{:S(2)}) collective-permute-start(f32[5,10,1,128]{3,2,1,0:T(1,128)S(1)} %get-tuple-element.118), channel_id=1, source_target_pairs={{4,0},{8,4},{12,8},{16,12},{20,16},{24,20},{28,24},{32,28},{36,32}... | collective-permute-start | bytes 76808 | tf_op jit(solution)/shard_map/ppermute | solution.py:23
  53.5 2.6 collective-permute-start.2
  56.5 4.0 %collective-permute-done.2 = f32[5,10,1,128]{3,2,1,0:T(1,128)S(1)} collective-permute-done((f32[5,10,1,128]{3,2,1,0:T(1,128)S(1)}, f32[5,10,1,128]{3,2,1,0:T(1,128)S(1)}, u32[]{:S(2)}, u32[]{:S(2)}) %collective-permute-start.2) | collective-permute-done | bytes 25632 | tf_op jit(solution)/shard_map/ppermute | solution.py:21
  60.8 3.5 %collective-permute-start.5 = (f32[5,10,10,1]{3,2,1,0:T(8,128)S(1)}, f32[5,10,10,1]{3,2,1,0:T(8,128)S(1)}, u32[]{:S(2)}, u32[]{:S(2)}) collective-permute-start(f32[5,10,10,1]{3,2,1,0:T(8,128)S(1)} %get-tuple-element.82), channel_id=1, source_target_pairs={{1,0},{2,1},{3,2},{0,3},{5,4},{6,5},{7,6},{4,7},{9,8},{10,9},{11,1... | collective-permute-start | bytes 6008 | tf_op jit(solution)/shard_map/ppermute | solution.py:23
  64.3 1.9 collective-permute-start.4
  66.7 6.4 %collective-permute-done.5 = f32[5,10,10,1]{3,2,1,0:T(8,128)S(1)} collective-permute-done((f32[5,10,10,1]{3,2,1,0:T(8,128)S(1)}, f32[5,10,10,1]{3,2,1,0:T(8,128)S(1)}, u32[]{:S(2)}, u32[]{:S(2)}) %collective-permute-start.5) | collective-permute-done | bytes 2032 | tf_op jit(solution)/shard_map/ppermute | solution.py:23
  73.1 2.0 collective-permute-done.4
  78.3 4.2 %collective-permute-start.7 = (f32[5,1,8,128]{3,2,1,0:T(8,128)}, f32[5,1,8,128]{3,2,1,0:T(8,128)S(1)}, u32[]{:S(2)}, u32[]{:S(2)}) collective-permute-start(f32[5,1,8,128]{3,2,1,0:T(8,128)} %get-tuple-element.131), channel_id=1, source_target_pairs={{64,0},{128,64},{192,128},{256,192},{320,256},{384,320},{448,384},... | collective-permute-start | bytes 61448 | tf_op jit(solution)/shard_map/ppermute | solution.py:23
  82.5 1.9 collective-permute-start.6
  87.6 0.8 slice_divide_fusion.8
  88.3 0.8 copy.298
  89.2 9.5 %all-to-all-start.1 = ((f32[16,2,1536]{2,1,0:T(2,128)}), f32[16,2,1536]{2,1,0:T(2,128)}, u32[]{:S(2)}, u32[]{:S(2)}) async-start(f32[16,2,1536]{2,1,0:T(2,128)} %copy.298), calls=%async_computation.1 | async-start | bytes 393216 | tf_op jit(solution)/shard_map/all_to_all | solution.py:211
  98.7 5.0 %collective-permute-start.9 = (f32[5,10,1,128]{3,2,1,0:T(1,128)S(1)}, f32[5,10,1,128]{3,2,1,0:T(1,128)S(1)}, u32[]{:S(2)}, u32[]{:S(2)}) collective-permute-start(f32[5,10,1,128]{3,2,1,0:T(1,128)S(1)} %get-tuple-element.113), channel_id=1, source_target_pairs={{4,0},{8,4},{12,8},{16,12},{20,16},{24,20},{28,24},{32,28},{36,32}... | collective-permute-start | bytes 76808 | tf_op jit(solution)/shard_map/ppermute | solution.py:23
  103.7 1.9 collective-permute-start.8
  106.0 0.9 collective-permute-done.9
  106.8 4.1 %collective-permute-done.8 = f32[5,10,1,128]{3,2,1,0:T(1,128)S(1)} collective-permute-done((f32[5,10,1,128]{3,2,1,0:T(1,128)S(1)}, f32[5,10,1,128]{3,2,1,0:T(1,128)S(1)}, u32[]{:S(2)}, u32[]{:S(2)}) %collective-permute-start.8) | collective-permute-done | bytes 25632 | tf_op jit(solution)/shard_map/ppermute | solution.py:21
  111.2 1.9 collective-permute-start.10
  113.1 5.3 %collective-permute-start.11 = (f32[5,10,10,1]{3,2,1,0:T(8,128)S(1)}, f32[5,10,10,1]{3,2,1,0:T(8,128)S(1)}, u32[]{:S(2)}, u32[]{:S(2)}) collective-permute-start(f32[5,10,10,1]{3,2,1,0:T(8,128)S(1)} %get-tuple-element.80), channel_id=1, source_target_pairs={{1,0},{2,1},{3,2},{0,3},{5,4},{6,5},{7,6},{4,7},{9,8},{10,9},{11,1... | collective-permute-start | bytes 6008 | tf_op jit(solution)/shard_map/ppermute | solution.py:23
  119.0 3.0 %collective-permute-done.10 = f32[5,10,10,1]{3,2,1,0:T(8,128)S(1)} collective-permute-done((f32[5,10,10,1]{3,2,1,0:T(8,128)S(1)}, f32[5,10,10,1]{3,2,1,0:T(8,128)S(1)}, u32[]{:S(2)}, u32[]{:S(2)}) %collective-permute-start.10) | collective-permute-done | bytes 2032 | tf_op jit(solution)/shard_map/ppermute | solution.py:21
  122.0 3.3 %collective-permute-done.11 = f32[5,10,10,1]{3,2,1,0:T(8,128)S(1)} collective-permute-done((f32[5,10,10,1]{3,2,1,0:T(8,128)S(1)}, f32[5,10,10,1]{3,2,1,0:T(8,128)S(1)}, u32[]{:S(2)}, u32[]{:S(2)}) %collective-permute-start.11) | collective-permute-done | bytes 2032 | tf_op jit(solution)/shard_map/ppermute | solution.py:23
  127.1 5.7 %collective-permute-start.13 = (f32[5,1,8,128]{3,2,1,0:T(8,128)S(1)}, f32[5,1,8,128]{3,2,1,0:T(8,128)S(1)}, u32[]{:S(2)}, u32[]{:S(2)}) collective-permute-start(f32[5,1,8,128]{3,2,1,0:T(8,128)S(1)} %get-tuple-element.129), channel_id=1, source_target_pairs={{64,0},{128,64},{192,128},{256,192},{320,256},{384,320},{448,384},... | collective-permute-start | bytes 61448 | tf_op jit(solution)/shard_map/ppermute | solution.py:23
  132.8 1.9 collective-permute-start.12
  138.5 0.8 copy.334
  140.7 2.2 collective-permute-start.15
  142.8 3.7 %collective-permute-start.14 = (f32[5,10,1,128]{3,2,1,0:T(1,128)}, f32[5,10,1,128]{3,2,1,0:T(1,128)S(1)}, u32[]{:S(2)}, u32[]{:S(2)}) collective-permute-start(f32[5,10,1,128]{3,2,1,0:T(1,128)} %get-tuple-element.107), channel_id=1, source_target_pairs={{0,4},{4,8},{8,12},{12,16},{16,20},{20,24},{24,28},{28,32},{32,36}... | collective-permute-start | bytes 76808 | tf_op jit(solution)/shard_map/ppermute | solution.py:21
  146.8 2.2 copy.272
  149.1 2.2 copy.270
  151.3 2.1 pad_maximum_fusion
  161.0 0.9 copy.387
  162.2 2.0 collective-permute-start.16
  164.2 5.3 %collective-permute-start.17 = (f32[5,10,10,1]{3,2,1,0:T(8,128)S(1)}, f32[5,10,10,1]{3,2,1,0:T(8,128)S(1)}, u32[]{:S(2)}, u32[]{:S(2)}) collective-permute-start(f32[5,10,10,1]{3,2,1,0:T(8,128)S(1)} %get-tuple-element.78), channel_id=1, source_target_pairs={{1,0},{2,1},{3,2},{0,3},{5,4},{6,5},{7,6},{4,7},{9,8},{10,9},{11,1... | collective-permute-start | bytes 6008 | tf_op jit(solution)/shard_map/ppermute | solution.py:23
  169.9 0.8 fusion.12
  170.7 2.4 collective-permute-done.16
  173.2 2.1 collective-permute-done.17
  179.4 1.1 reshape_reshape.82
  180.5 1.2 convolution_bitcast_fusion.3
  182.5 1.0 multiply_add_fusion
  183.6 0.8 copy.369
  185.4 0.8 fusion.82
  186.2 9.4 %all-to-all-start.2 = ((f32[16,2,1536]{2,1,0:T(2,128)}), f32[16,2,1536]{2,1,0:T(2,128)S(1)}, u32[]{:S(2)}, u32[]{:S(2)}) async-start(f32[16,2,1536]{2,1,0:T(2,128)} %copy.334), calls=%async_computation.2 | async-start | bytes 393216 | tf_op jit(solution)/shard_map/all_to_all | solution.py:211
  195.6 1.1 reshape.513
  197.4 10.9 %collective-permute-start.21 = (f32[16,4,512]{2,0,1:T(8,128)S(1)}, f32[16,4,512]{2,0,1:T(8,128)S(1)}, u32[]{:S(2)}, u32[]{:S(2)}) collective-permute-start(f32[16,4,512]{2,0,1:T(8,128)S(1)} %fusion.92), channel_id=1, source_target_pairs={{1,0},{2,1},{3,2},{4,3},{5,4},{6,5},{7,6},{8,7},{9,8},{10,9},{11,1... | collective-permute-start | bytes 393224 | tf_op jit(solution)/shard_map/ppermute | solution.py:23
  208.3 1.9 collective-permute-start.20
  211.1 7.2 %all-to-all-start.3 = ((f32[16,2,1536]{2,1,0:T(2,128)}), f32[16,2,1536]{2,1,0:T(2,128)S(1)}, u32[]{:S(2)}, u32[]{:S(2)}) async-start(f32[16,2,1536]{2,1,0:T(2,128)} %copy.369), calls=%async_computation.3 | async-start | bytes 393216 | tf_op jit(solution)/shard_map/all_to_all | solution.py:211
  219.3 14.8 %all-to-all-done.3 = f32[16,2,1536]{2,1,0:T(2,128)S(1)} async-done(((f32[16,2,1536]{2,1,0:T(2,128)}), f32[16,2,1536]{2,1,0:T(2,128)S(1)}, u32[]{:S(2)}, u32[]{:S(2)}) %all-to-all-start.3) | async-done | bytes 196640 | tf_op jit(solution)/shard_map/all_to_all | solution.py:211
  243.9 11.2 %collective-permute-start.23 = (f32[16,4,512]{2,0,1:T(8,128)S(1)}, f32[16,4,512]{2,0,1:T(8,128)S(1)}, u32[]{:S(2)}, u32[]{:S(2)}) collective-permute-start(f32[16,4,512]{2,0,1:T(8,128)S(1)} %fusion.95), channel_id=1, source_target_pairs={{1,0},{2,1},{3,2},{4,3},{5,4},{6,5},{7,6},{8,7},{9,8},{10,9},{11,1... | collective-permute-start | bytes 393224 | tf_op jit(solution)/shard_map/ppermute | solution.py:23
  255.1 2.2 collective-permute-start.22
  258.3 7.6 %collective-permute-done.22 = f32[16,4,512]{2,0,1:T(8,128)S(1)} collective-permute-done((f32[16,4,512]{2,0,1:T(8,128)S(1)}, f32[16,4,512]{2,0,1:T(8,128)S(1)}, u32[]{:S(2)}, u32[]{:S(2)}) %collective-permute-start.22) | collective-permute-done | bytes 131104 | tf_op jit(solution)/shard_map/ppermute | solution.py:21
  274.1 0.7 copy.372
  (386 shorter events, 61.6 us)
Async XLA Ops:
  0.6 36.6 %copy-start.1 = (f32[16,4,512]{2,1,0:T(4,128)S(1)}, f32[16,4,512]{2,1,0:T(4,128)}, u32[]{:S(2)}) copy-start(f32[16,4,512]{2,1,0:T(4,128)} %param.13) | copy-start | bytes 393220
  0.6 36.7 %copy-start.15 = (f32[8,8]{1,0:T(8,128)S(1)}, f32[8,8]{1,0:T(8,128)}, u32[]{:S(2)}) copy-start(f32[8,8]{1,0:T(8,128)} %param.16) | copy-start | bytes 772
  0.7 36.8 %copy-start.16 = (f32[8,8]{1,0:T(8,128)S(1)}, f32[8,8]{1,0:T(8,128)}, u32[]{:S(2)}) copy-start(f32[8,8]{1,0:T(8,128)} %param.15) | copy-start | bytes 772
  2.3 144.5 %collective-permute-start.19 = (f32[16,4,512]{2,0,1:T(8,128)}, f32[16,4,512]{2,0,1:T(8,128)}, u32[]{:S(2)}, u32[]{:S(2)}) collective-permute-start(f32[16,4,512]{2,0,1:T(8,128)} %copy.259), channel_id=1, source_target_pairs={{1,0},{2,1},{3,2},{4,3},{5,4},{6,5},{7,6},{8,7},{9,8},{10,9},{11,1... | collective-permute-start | bytes 393224 | tf_op jit(solution)/shard_map/ppermute | solution.py:23
  15.8 133.3 %collective-permute-start.18 = (f32[16,4,512]{2,0,1:T(8,128)}, f32[16,4,512]{2,0,1:T(8,128)}, u32[]{:S(2)}, u32[]{:S(2)}) collective-permute-start(f32[16,4,512]{2,0,1:T(8,128)} %copy.259), channel_id=1, source_target_pairs={{0,1},{1,2},{2,3},{3,4},{4,5},{5,6},{6,7},{7,8},{8,9},{9,10},{10,1... | collective-permute-start | bytes 393224 | tf_op jit(solution)/shard_map/ppermute | solution.py:21
  20.2 30.0 %collective-permute-start.1 = (f32[5,1,8,128]{3,2,1,0:T(8,128)S(1)}, f32[5,1,8,128]{3,2,1,0:T(8,128)S(1)}, u32[]{:S(2)}, u32[]{:S(2)}) collective-permute-start(f32[5,1,8,128]{3,2,1,0:T(8,128)S(1)} %get-tuple-element.133), channel_id=1, source_target_pairs={{64,0},{128,64},{192,128},{256,192},{320,256},{384,320},{448,384},... | collective-permute-start | bytes 61448 | tf_op jit(solution)/shard_map/ppermute | solution.py:23
  22.1 28.1 %collective-permute-start = (f32[5,1,8,128]{3,2,1,0:T(8,128)S(1)}, f32[5,1,8,128]{3,2,1,0:T(8,128)S(1)}, u32[]{:S(2)}, u32[]{:S(2)}) collective-permute-start(f32[5,1,8,128]{3,2,1,0:T(8,128)S(1)} %get-tuple-element.132), channel_id=1, source_target_pairs={{0,64},{64,128},{128,192},{192,256},{256,320},{320,384},{384,448},... | collective-permute-start | bytes 61448 | tf_op jit(solution)/shard_map/ppermute | solution.py:21
  28.3 7.8 %copy-start.20 = (s32[16]{0:T(128)}, s32[16]{0:T(128)S(1)}, u32[]{:S(2)}) copy-start(s32[16]{0:T(128)S(1)} %multiply_add_fusion.10) | copy-start | bytes 196
  29.8 18.7 %all-to-all-start = ((s32[16,1,2]{2,1,0:T(1,128)}), s32[16,1,2]{2,1,0:T(1,128)S(1)}, u32[]{:S(2)}, u32[]{:S(2)}) async-start(s32[16,1,2]{2,1,0:T(1,128)} %bitcast.80), calls=%async_computation | async-start | bytes 16384 | tf_op jit(solution)/shard_map/all_to_all | solution.py:212
  36.1 39.8 %copy-start.23 = (f32[3]{0:T(128)}, f32[3]{0:T(128)S(1)}, u32[]{:S(2)}) copy-start(f32[3]{0:T(128)S(1)} %compare_convert_fusion) | copy-start | bytes 40
  36.1 30.2 %copy-start.26 = (f32[3]{0:T(128)}, f32[3]{0:T(128)S(1)}, u32[]{:S(2)}) copy-start(f32[3]{0:T(128)S(1)} %compare_convert_fusion.1) | copy-start | bytes 40
  38.4 2.2 copy-start.30
  38.4 2.2 copy-start.31
  39.8 10.5 %copy-start = (f32[8,8,128]{2,1,0:T(8,128)S(1)}, f32[8,8,128]{2,1,0:T(8,128)}, u32[]{:S(2)}) copy-start(f32[8,8,128]{2,1,0:T(8,128)} %param.10) | copy-start | bytes 98308
  43.6 12.7 %copy-start.28 = (f32[3]{0:T(128)}, f32[3]{0:T(128)S(1)}, u32[]{:S(2)}) copy-start(f32[3]{0:T(128)S(1)} %compare_convert_fusion.2) | copy-start | bytes 40
  50.3 6.2 %collective-permute-start.3 = (f32[5,10,1,128]{3,2,1,0:T(1,128)S(1)}, f32[5,10,1,128]{3,2,1,0:T(1,128)S(1)}, u32[]{:S(2)}, u32[]{:S(2)}) collective-permute-start(f32[5,10,1,128]{3,2,1,0:T(1,128)S(1)} %get-tuple-element.118), channel_id=1, source_target_pairs={{4,0},{8,4},{12,8},{16,12},{20,16},{24,20},{28,24},{32,28},{36,32}... | collective-permute-start | bytes 76808 | tf_op jit(solution)/shard_map/ppermute | solution.py:23
  53.5 6.9 %collective-permute-start.2 = (f32[5,10,1,128]{3,2,1,0:T(1,128)S(1)}, f32[5,10,1,128]{3,2,1,0:T(1,128)S(1)}, u32[]{:S(2)}, u32[]{:S(2)}) collective-permute-start(f32[5,10,1,128]{3,2,1,0:T(1,128)S(1)} %get-tuple-element.117), channel_id=1, source_target_pairs={{0,4},{4,8},{8,12},{12,16},{16,20},{20,24},{24,28},{28,32},{32,36}... | collective-permute-start | bytes 76808 | tf_op jit(solution)/shard_map/ppermute | solution.py:21
  60.8 12.3 %collective-permute-start.5 = (f32[5,10,10,1]{3,2,1,0:T(8,128)S(1)}, f32[5,10,10,1]{3,2,1,0:T(8,128)S(1)}, u32[]{:S(2)}, u32[]{:S(2)}) collective-permute-start(f32[5,10,10,1]{3,2,1,0:T(8,128)S(1)} %get-tuple-element.82), channel_id=1, source_target_pairs={{1,0},{2,1},{3,2},{0,3},{5,4},{6,5},{7,6},{4,7},{9,8},{10,9},{11,1... | collective-permute-start | bytes 6008 | tf_op jit(solution)/shard_map/ppermute | solution.py:23
  64.3 10.8 %collective-permute-start.4 = (f32[5,10,10,1]{3,2,1,0:T(8,128)S(1)}, f32[5,10,10,1]{3,2,1,0:T(8,128)S(1)}, u32[]{:S(2)}, u32[]{:S(2)}) collective-permute-start(f32[5,10,10,1]{3,2,1,0:T(8,128)S(1)} %get-tuple-element.83), channel_id=1, source_target_pairs={{0,1},{1,2},{2,3},{3,0},{4,5},{5,6},{6,7},{7,4},{8,9},{9,10},{10,1... | collective-permute-start | bytes 6008 | tf_op jit(solution)/shard_map/ppermute | solution.py:21
  78.3 20.3 %collective-permute-start.7 = (f32[5,1,8,128]{3,2,1,0:T(8,128)}, f32[5,1,8,128]{3,2,1,0:T(8,128)S(1)}, u32[]{:S(2)}, u32[]{:S(2)}) collective-permute-start(f32[5,1,8,128]{3,2,1,0:T(8,128)} %get-tuple-element.131), channel_id=1, source_target_pairs={{64,0},{128,64},{192,128},{256,192},{320,256},{384,320},{448,384},... | collective-permute-start | bytes 61448 | tf_op jit(solution)/shard_map/ppermute | solution.py:23
  82.5 16.2 %collective-permute-start.6 = (f32[5,1,8,128]{3,2,1,0:T(8,128)S(1)}, f32[5,1,8,128]{3,2,1,0:T(8,128)S(1)}, u32[]{:S(2)}, u32[]{:S(2)}) collective-permute-start(f32[5,1,8,128]{3,2,1,0:T(8,128)S(1)} %get-tuple-element.130), channel_id=1, source_target_pairs={{0,64},{64,128},{128,192},{192,256},{256,320},{320,384},{384,448},... | collective-permute-start | bytes 61448 | tf_op jit(solution)/shard_map/ppermute | solution.py:21
  86.1 0.8 copy-start.3
  86.1 1.2 copy-start.21
  87.2 18.6 %copy-start.29 = (f32[3]{0:T(128)S(1)}, f32[3]{0:T(128)}, u32[]{:S(2)}) copy-start(f32[3]{0:T(128)} %copy-done.28) | copy-start | bytes 40
  89.2 97.0 %all-to-all-start.1 = ((f32[16,2,1536]{2,1,0:T(2,128)}), f32[16,2,1536]{2,1,0:T(2,128)}, u32[]{:S(2)}, u32[]{:S(2)}) async-start(f32[16,2,1536]{2,1,0:T(2,128)} %copy.298), calls=%async_computation.1 | async-start | bytes 393216 | tf_op jit(solution)/shard_map/all_to_all | solution.py:211
  98.7 8.1 %collective-permute-start.9 = (f32[5,10,1,128]{3,2,1,0:T(1,128)S(1)}, f32[5,10,1,128]{3,2,1,0:T(1,128)S(1)}, u32[]{:S(2)}, u32[]{:S(2)}) collective-permute-start(f32[5,10,1,128]{3,2,1,0:T(1,128)S(1)} %get-tuple-element.113), channel_id=1, source_target_pairs={{4,0},{8,4},{12,8},{16,12},{20,16},{24,20},{28,24},{32,28},{36,32}... | collective-permute-start | bytes 76808 | tf_op jit(solution)/shard_map/ppermute | solution.py:23
  103.7 7.2 %collective-permute-start.8 = (f32[5,10,1,128]{3,2,1,0:T(1,128)S(1)}, f32[5,10,1,128]{3,2,1,0:T(1,128)S(1)}, u32[]{:S(2)}, u32[]{:S(2)}) collective-permute-start(f32[5,10,1,128]{3,2,1,0:T(1,128)S(1)} %get-tuple-element.112), channel_id=1, source_target_pairs={{0,4},{4,8},{8,12},{12,16},{16,20},{20,24},{24,28},{28,32},{32,36}... | collective-permute-start | bytes 76808 | tf_op jit(solution)/shard_map/ppermute | solution.py:21
  111.0 7.6 %copy-start.27 = (f32[3]{0:T(128)S(1)}, f32[3]{0:T(128)}, u32[]{:S(2)}) copy-start(f32[3]{0:T(128)} %copy-done.26) | copy-start | bytes 40
  111.2 10.8 %collective-permute-start.10 = (f32[5,10,10,1]{3,2,1,0:T(8,128)S(1)}, f32[5,10,10,1]{3,2,1,0:T(8,128)S(1)}, u32[]{:S(2)}, u32[]{:S(2)}) collective-permute-start(f32[5,10,10,1]{3,2,1,0:T(8,128)S(1)} %get-tuple-element.81), channel_id=1, source_target_pairs={{0,1},{1,2},{2,3},{3,0},{4,5},{5,6},{6,7},{7,4},{8,9},{9,10},{10,1... | collective-permute-start | bytes 6008 | tf_op jit(solution)/shard_map/ppermute | solution.py:21
  113.1 12.2 %collective-permute-start.11 = (f32[5,10,10,1]{3,2,1,0:T(8,128)S(1)}, f32[5,10,10,1]{3,2,1,0:T(8,128)S(1)}, u32[]{:S(2)}, u32[]{:S(2)}) collective-permute-start(f32[5,10,10,1]{3,2,1,0:T(8,128)S(1)} %get-tuple-element.80), channel_id=1, source_target_pairs={{1,0},{2,1},{3,2},{0,3},{5,4},{6,5},{7,6},{4,7},{9,8},{10,9},{11,1... | collective-permute-start | bytes 6008 | tf_op jit(solution)/shard_map/ppermute | solution.py:23
  125.6 0.6 copy-start.24
  127.1 12.2 %collective-permute-start.13 = (f32[5,1,8,128]{3,2,1,0:T(8,128)S(1)}, f32[5,1,8,128]{3,2,1,0:T(8,128)S(1)}, u32[]{:S(2)}, u32[]{:S(2)}) collective-permute-start(f32[5,1,8,128]{3,2,1,0:T(8,128)S(1)} %get-tuple-element.129), channel_id=1, source_target_pairs={{64,0},{128,64},{192,128},{256,192},{320,256},{384,320},{448,384},... | collective-permute-start | bytes 61448 | tf_op jit(solution)/shard_map/ppermute | solution.py:23
  132.8 7.2 %collective-permute-start.12 = (f32[5,1,8,128]{3,2,1,0:T(8,128)S(1)}, f32[5,1,8,128]{3,2,1,0:T(8,128)S(1)}, u32[]{:S(2)}, u32[]{:S(2)}) collective-permute-start(f32[5,1,8,128]{3,2,1,0:T(8,128)S(1)} %get-tuple-element.128), channel_id=1, source_target_pairs={{0,64},{64,128},{128,192},{192,256},{256,320},{320,384},{384,448},... | collective-permute-start | bytes 61448 | tf_op jit(solution)/shard_map/ppermute | solution.py:21
  136.4 0.8 copy-start.4
  136.4 1.2 copy-start.22
  140.7 21.3 %collective-permute-start.15 = (f32[5,10,1,128]{3,2,1,0:T(1,128)}, f32[5,10,1,128]{3,2,1,0:T(1,128)S(1)}, u32[]{:S(2)}, u32[]{:S(2)}) collective-permute-start(f32[5,10,1,128]{3,2,1,0:T(1,128)} %get-tuple-element.108), channel_id=1, source_target_pairs={{4,0},{8,4},{12,8},{16,12},{20,16},{24,20},{28,24},{32,28},{36,32}... | collective-permute-start | bytes 76808 | tf_op jit(solution)/shard_map/ppermute | solution.py:23
  142.8 19.1 %collective-permute-start.14 = (f32[5,10,1,128]{3,2,1,0:T(1,128)}, f32[5,10,1,128]{3,2,1,0:T(1,128)S(1)}, u32[]{:S(2)}, u32[]{:S(2)}) collective-permute-start(f32[5,10,1,128]{3,2,1,0:T(1,128)} %get-tuple-element.107), channel_id=1, source_target_pairs={{0,4},{4,8},{8,12},{12,16},{16,20},{20,24},{24,28},{28,32},{32,36}... | collective-permute-start | bytes 76808 | tf_op jit(solution)/shard_map/ppermute | solution.py:21
  159.5 1.2 copy-start.18
  160.1 0.8 copy-start.12
  160.1 0.8 copy-start.13
  160.1 0.8 copy-start.14
  162.2 11.0 %collective-permute-start.16 = (f32[5,10,10,1]{3,2,1,0:T(8,128)S(1)}, f32[5,10,10,1]{3,2,1,0:T(8,128)S(1)}, u32[]{:S(2)}, u32[]{:S(2)}) collective-permute-start(f32[5,10,10,1]{3,2,1,0:T(8,128)S(1)} %get-tuple-element.79), channel_id=1, source_target_pairs={{0,1},{1,2},{2,3},{3,0},{4,5},{5,6},{6,7},{7,4},{8,9},{9,10},{10,1... | collective-permute-start | bytes 6008 | tf_op jit(solution)/shard_map/ppermute | solution.py:21
  164.2 11.1 %collective-permute-start.17 = (f32[5,10,10,1]{3,2,1,0:T(8,128)S(1)}, f32[5,10,10,1]{3,2,1,0:T(8,128)S(1)}, u32[]{:S(2)}, u32[]{:S(2)}) collective-permute-start(f32[5,10,10,1]{3,2,1,0:T(8,128)S(1)} %get-tuple-element.78), channel_id=1, source_target_pairs={{1,0},{2,1},{3,2},{0,3},{5,4},{6,5},{7,6},{4,7},{9,8},{10,9},{11,1... | collective-permute-start | bytes 6008 | tf_op jit(solution)/shard_map/ppermute | solution.py:23
  175.6 2.2 copy-start.5
  179.4 3.1 %copy-start.25 = (f32[3]{0:T(128)S(1)}, f32[3]{0:T(128)}, u32[]{:S(2)}) copy-start(f32[3]{0:T(128)} %copy-done.23) | copy-start | bytes 40
  180.5 2.9 %copy-start.8 = (f32[1,8,8,130]{3,2,1,0:T(8,128)S(1)}, f32[1,8,8,130]{3,2,1,0:T(8,128)}, u32[]{:S(2)}) copy-start(f32[1,8,8,130]{3,2,1,0:T(8,128)} %get-tuple-element.157) | copy-start | bytes 99844
  183.4 1.2 copy-start.7
  184.4 1.0 copy-start.2
  185.4 11.4 %copy-start.6 = (f32[16,3,512]{2,0,1:T(8,128)S(1)}, f32[16,3,512]{2,0,1:T(8,128)}, u32[]{:S(2)}) copy-start(f32[16,3,512]{2,0,1:T(8,128)} %copy.387) | copy-start | bytes 294916
  185.4 11.4 %copy-start.9 = (f32[16,1,512]{2,0,1:T(8,128)S(1)}, f32[16,1,512]{2,0,1:T(8,128)}, u32[]{:S(2)}) copy-start(f32[16,1,512]{2,0,1:T(8,128)} %copy.386) | copy-start | bytes 98308
  185.4 11.4 %copy-start.10 = (f32[16,1,512]{2,0,1:T(8,128)S(1)}, f32[16,1,512]{2,0,1:T(8,128)}, u32[]{:S(2)}) copy-start(f32[16,1,512]{2,0,1:T(8,128)} %copy.385) | copy-start | bytes 98308
  185.4 11.4 %copy-start.11 = (f32[16,1,512]{2,0,1:T(8,128)S(1)}, f32[16,1,512]{2,0,1:T(8,128)}, u32[]{:S(2)}) copy-start(f32[16,1,512]{2,0,1:T(8,128)} %copy.384) | copy-start | bytes 98308
  185.4 11.4 %copy-start.17 = (s32[32]{0:T(128)S(1)}, s32[32]{0:T(128)}, u32[]{:S(2)}) copy-start(s32[32]{0:T(128)} %eq.169) | copy-start | bytes 388
  186.2 24.9 %all-to-all-start.2 = ((f32[16,2,1536]{2,1,0:T(2,128)}), f32[16,2,1536]{2,1,0:T(2,128)S(1)}, u32[]{:S(2)}, u32[]{:S(2)}) async-start(f32[16,2,1536]{2,1,0:T(2,128)} %copy.334), calls=%async_computation.2 | async-start | bytes 393216 | tf_op jit(solution)/shard_map/all_to_all | solution.py:211
  197.4 36.9 %collective-permute-start.21 = (f32[16,4,512]{2,0,1:T(8,128)S(1)}, f32[16,4,512]{2,0,1:T(8,128)S(1)}, u32[]{:S(2)}, u32[]{:S(2)}) collective-permute-start(f32[16,4,512]{2,0,1:T(8,128)S(1)} %fusion.92), channel_id=1, source_target_pairs={{1,0},{2,1},{3,2},{4,3},{5,4},{6,5},{7,6},{8,7},{9,8},{10,9},{11,1... | collective-permute-start | bytes 393224 | tf_op jit(solution)/shard_map/ppermute | solution.py:23
  208.3 26.0 %collective-permute-start.20 = (f32[16,4,512]{2,0,1:T(8,128)S(1)}, f32[16,4,512]{2,0,1:T(8,128)S(1)}, u32[]{:S(2)}, u32[]{:S(2)}) collective-permute-start(f32[16,4,512]{2,0,1:T(8,128)S(1)} %fusion.92), channel_id=1, source_target_pairs={{0,1},{1,2},{2,3},{3,4},{4,5},{5,6},{6,7},{7,8},{8,9},{9,10},{10,1... | collective-permute-start | bytes 393224 | tf_op jit(solution)/shard_map/ppermute | solution.py:21
  211.1 23.1 %all-to-all-start.3 = ((f32[16,2,1536]{2,1,0:T(2,128)}), f32[16,2,1536]{2,1,0:T(2,128)S(1)}, u32[]{:S(2)}, u32[]{:S(2)}) async-start(f32[16,2,1536]{2,1,0:T(2,128)} %copy.369), calls=%async_computation.3 | async-start | bytes 393216 | tf_op jit(solution)/shard_map/all_to_all | solution.py:211
  241.8 0.7 copy-start.19
  243.9 14.4 %collective-permute-start.23 = (f32[16,4,512]{2,0,1:T(8,128)S(1)}, f32[16,4,512]{2,0,1:T(8,128)S(1)}, u32[]{:S(2)}, u32[]{:S(2)}) collective-permute-start(f32[16,4,512]{2,0,1:T(8,128)S(1)} %fusion.95), channel_id=1, source_target_pairs={{1,0},{2,1},{3,2},{4,3},{5,4},{6,5},{7,6},{8,7},{9,8},{10,9},{11,1... | collective-permute-start | bytes 393224 | tf_op jit(solution)/shard_map/ppermute | solution.py:23
  255.1 10.8 %collective-permute-start.22 = (f32[16,4,512]{2,0,1:T(8,128)S(1)}, f32[16,4,512]{2,0,1:T(8,128)S(1)}, u32[]{:S(2)}, u32[]{:S(2)}) collective-permute-start(f32[16,4,512]{2,0,1:T(8,128)S(1)} %fusion.95), channel_id=1, source_target_pairs={{0,1},{1,2},{2,3},{3,4},{4,5},{5,6},{6,7},{7,8},{8,9},{9,10},{10,1... | collective-permute-start | bytes 393224 | tf_op jit(solution)/shard_map/ppermute | solution.py:21
where the time goes:
time: 277 us; the launch traced here: 275 us
  starting transfers between devices  132 us (48%)
  waiting for transfers between devices  53.2 us (19%)
  local copies, waits for them, and re-layouts  49.8 us (18%)
  other arithmetic  29.3 us (11%)
  matrix products  7.5 us (3%)
  between operations  2.97 us (1%)
    ppermute x12, starting transfers between devices, padded_2(): lax.ppermute(head, axis, [((i + 1) % count, i) for i in range(ends)])  71.9 us
    ppermute x12, starting transfers between devices, padded_2(): lax.ppermute(tail, axis, [(i, (i + 1) % count) for i in range(ends)])  27.9 us
    all_to_all x3, starting transfers between devices, route(): lax.all_to_all(packed, 'fy', split_axis=0, concat_axis=0, tiled=True)  26.2 us
    ppermute x12, waiting for transfers between devices, padded_2(): lax.ppermute(tail, axis, [(i, (i + 1) % count) for i in range(ends)])  23.8 us
    all_to_all x3, waiting for transfers between devices, route(): lax.all_to_all(packed, 'fy', split_axis=0, concat_axis=0, tiled=True)  14.8 us
    gather x36, local copies, waits for them, and re-layouts, face_jumps(): face_table[:, :, opposite * 64:(opposite + 1) * 64]  14.5 us
    ppermute x12, waiting for transfers between devices, padded_2(): lax.ppermute(head, axis, [((i + 1) % count, i) for i in range(ends)])  12.7 us
    unnamed x82, local copies, waits for them, and re-layouts  7.46 us
  transfers between devices with their start and end apart: 28, of which 13 were waited for; matrix products, arithmetic and copies ran while one was open for 24% of the time, Pallas kernels for 0%

commit v1 on v0

v1 whole, which is shorter than its diff:
```python
import functools

import jax
import jax.numpy as jnp
from jax import lax
from jax.experimental import pallas as pl
from jax.experimental.pallas import tpu as pltpu
from jax.sharding import PartitionSpec as P

HEAT_RATIO = 1.4
TIME_STEP = 0.1
VISCOSITY = 0.05
PENALTY = 0.5
HIGHEST = lax.Precision.HIGHEST
MESH = pl.DeviceIdType.MESH
BLEND = ((0.0, 1.0), (0.75, 0.25), (1.0 / 3.0, 2.0 / 3.0))
F32 = jnp.float32
BF16 = jnp.bfloat16


def dot(a, b):
    return jnp.dot(a, b, precision=HIGHEST, preferred_element_type=F32)


def dot_nt(a, b):
    return lax.dot_general(
        a, b, (((1,), (1,)), ((), ())), precision=HIGHEST, preferred_element_type=F32
    )


def dot_tn(a, b):
    return lax.dot_general(
        a, b, (((0,), (0,)), ((), ())), precision=HIGHEST, preferred_element_type=F32
    )


def pick(values, chooser):
    rows = values.shape[0]
    high = values.astype(BF16)
    rest = values - high.astype(F32)
    middle = rest.astype(BF16)
    low = (rest - middle.astype(F32)).astype(BF16)
    parts = jnp.dot(
        jnp.concatenate([high, middle, low], 0), chooser, preferred_element_type=F32
    )
    return parts[:rows] + parts[rows : 2 * rows] + parts[2 * rows :]


def iota(shape, dim):
    return lax.broadcasted_iota(jnp.int32, shape, dim)


def eighth(values):
    return lax.shift_right_logical(values, 3)


def repeat_rows(matrix, count, by_block, turned=False):
    rows, columns = iota((count, 8), 0), iota((count, 8), 1)
    chooser = ((eighth(rows) if by_block else rows & 7) == columns).astype(F32)
    if turned:
        return dot_nt(chooser, dot(chooser, matrix))
    return dot_nt(dot(chooser, matrix), chooser)


def swap_groups(values):
    rows, groups = iota((16, 128), 0), eighth(iota((16, 128), 1))
    for bit in range(4):
        step = 1 << bit
        row_bit, group_bit = (rows & step) != 0, (groups & step) != 0
        down = pltpu.roll(pltpu.roll(values, 16 - step, 1), 8 * step, 2)
        up = pltpu.roll(pltpu.roll(values, step, 1), 128 - 8 * step, 2)
        values = jnp.where(
            (row_bit == group_bit)[None], values, jnp.where(group_bit[None], down, up)
        )
    return values


def sweep(cells, along):
    density, momentum, energy = cells[0], cells[1:4], cells[4]
    inverse = 1.0 / density
    velocity = [part * inverse for part in momentum]
    kinetic = sum(part * speed for part, speed in zip(momentum, velocity))
    pressure = (HEAT_RATIO - 1.0) * (energy - 0.5 * kinetic)
    normal = velocity[along]
    signal = jnp.abs(normal) + jnp.sqrt(HEAT_RATIO * jnp.abs(pressure) * inverse)
    half_speed = 0.5 * jnp.maximum(signal[:-1], signal[1:])
    fluxes = [momentum[along]] + [part * normal for part in momentum] + [(energy + pressure) * normal]
    fluxes[1 + along] = fluxes[1 + along] + pressure
    rates = []
    for index, (flux, cell) in enumerate(zip(fluxes, cells)):
        gap = cell[1:] - cell[:-1]
        face = 0.5 * (flux[:-1] + flux[1:]) - half_speed * gap
        rate = face[:-1] - face[1:]
        if 1 <= index <= 3:
            rate = rate + VISCOSITY * (gap[1:] - gap[:-1])
        rates.append(rate)
    slopes = [0.5 * (velocity[c][2:] - velocity[c][:-2]) for c in range(3) if c != along]
    return rates + slopes


def kernel(
    sizes,
    density_ref,
    velocity_ref,
    pressure_ref,
    acoustic_ref,
    speed_ref,
    derivative_ref,
    basis_ref,
    neighbour_ref,
    owner_ref,
    element_ref,
    flow_out,
    sound_out,
    flow,
    halo_send,
    halo_recv,
    turned,
    sound,
    trace,
    trace_recv,
    rate_ref,
    packed,
    arrived,
    labels,
    labels_recv,
    gather_ref,
    place_ref,
    route_ref,
    pair_ref,
    slope_ref,
    slope_z_ref,
    halo_out_sem,
    halo_in_sem,
    trace_out_sem,
    trace_in_sem,
    packed_out_sem,
    packed_in_sem,
    label_out_sem,
    label_in_sem,
):
    n_x, n_y, n_z = sizes
    fx, fy, fz = lax.axis_index("fx"), lax.axis_index("fy"), lax.axis_index("fz")
    place = (fx * n_y + fy) * n_z + fz
    total = n_x * n_y * n_z

    def device_at(index):
        return (index // (n_y * n_z), (index // n_z) % n_y, index % n_z)

    after, before = device_at((place + 1) % total), device_at((place + total - 1) % total)
    beside = [
        ((fx + 1) % n_x, fy, fz),
        ((fx + n_x - 1) % n_x, fy, fz),
        (fx, (fy + 1) % n_y, fz),
        (fx, (fy + n_y - 1) % n_y, fz),
        (fx, fy, (fz + 1) % n_z),
        (fx, fy, (fz + n_z - 1) % n_z),
    ]
    barrier = pltpu.get_barrier_semaphore()
    for device in [beside[0], beside[1], beside[4], beside[5], after, before]:
        pl.semaphore_signal(barrier, inc=1, device_id=device, device_id_type=MESH)

    @pl.loop(1, n_y)
    def _(step):
        pl.semaphore_signal(
            barrier, inc=1, device_id=(fx, (fy + step) % n_y, fz), device_id_type=MESH
        )

    lane = iota((8, 128), 1)
    digit = lane & 7

    def pack_halos(stage):
        for side, row in ((0, 7), (1, 0)):
            halo_send[stage, side] = flow[stage, :, pl.ds(row, 8, stride=8), :]
        ends = [jnp.zeros((5, 8, 128), F32)] * 2
        for x in range(8):
            plane = flow[stage, :, 8 * x : 8 * x + 8, :]
            ends[0] = jnp.where(lane == x, pltpu.roll(plane, x + 1, 2), ends[0])
            ends[1] = jnp.where(lane == x, pltpu.roll(plane, x, 2) if x else plane, ends[1])
        halo_send[stage, 2], halo_send[stage, 3] = ends

    def halo_copies(stage):
        sources = [flow.at[stage, :, pl.ds(56, 8), :], flow.at[stage, :, pl.ds(0, 8), :]]
        sources += [halo_send.at[stage, index] for index in range(4)]
        return [
            pltpu.make_async_remote_copy(
                src_ref=source,
                dst_ref=halo_recv.at[stage, index],
                send_sem=halo_out_sem.at[stage, index],
                recv_sem=halo_in_sem.at[stage, index],
                device_id=beside[index],
                device_id_type=MESH,
            )
            for index, source in enumerate(sources)
        ]

    def take_traces(stage):
        trace[stage, 0, 0] = sound[stage, :, 0:8, :]
        trace[stage, 1, 0] = sound[stage, :, 56:64, :]
        trace[stage, 0, 1] = sound[stage, :, pl.ds(0, 8, stride=8), :]
        trace[stage, 1, 1] = sound[stage, :, pl.ds(7, 8, stride=8), :]
        ends = [jnp.zeros((4, 8, 128), F32)] * 2
        for x in range(8):
            plane = sound[stage, :, 8 * x : 8 * x + 8, :]
            ends[0] = jnp.where(digit == x, pltpu.roll(plane, x, 2) if x else plane, ends[0])
            ends[1] = jnp.where(digit == x, pltpu.roll(plane, 121 + x, 2) if x < 7 else plane, ends[1])
        trace[stage, 0, 2], trace[stage, 1, 2] = ends

    def trace_copies(stage):
        return [
            pltpu.make_async_remote_copy(
                src_ref=trace.at[stage, 1 - side],
                dst_ref=trace_recv.at[stage, side],
                send_sem=trace_out_sem.at[stage, side],
                recv_sem=trace_in_sem.at[stage, side],
                device_id=device,
                device_id_type=MESH,
            )
            for side, device in ((0, after), (1, before))
        ]

    def spread(source, target, out_sem, in_sem):
        @pl.loop(1, n_y)
        def _(step):
            peer = (fy + step) % n_y
            pltpu.make_async_remote_copy(
                src_ref=source.at[peer],
                dst_ref=target.at[fy],
                send_sem=out_sem,
                recv_sem=in_sem,
                device_id=(fx, peer, fz),
                device_id_type=MESH,
            ).start()

        target[fy] = source[fy]

    def spread_whole(source, target, out_sem, in_sem):
        return pltpu.make_async_remote_copy(
            src_ref=source.at[pl.ds(0, n_y - 1)],
            dst_ref=target.at[pl.ds(0, n_y - 1)],
            send_sem=out_sem,
            recv_sem=in_sem,
            device_id=beside[2],
            device_id_type=MESH,
        )

    def label_args():
        return (labels, labels_recv, label_out_sem.at[0], label_in_sem.at[0])

    def packet_args(stage):
        return (
            packed.at[stage],
            arrived.at[stage],
            packed_out_sem.at[stage],
            packed_in_sem.at[stage],
        )

    density = density_ref[...].reshape(64, 128)
    speeds = velocity_ref[...].reshape(3, 64, 128)
    energy = pressure_ref[...].reshape(64, 128) / (HEAT_RATIO - 1.0) + 0.5 * density * (
        speeds[0] * speeds[0] + speeds[1] * speeds[1] + speeds[2] * speeds[2]
    )
    flow[0, 0] = density
    for part in range(3):
        flow[0, 1 + part] = density * speeds[part]
    flow[0, 4] = energy
    pack_halos(0)

    pl.semaphore_wait(barrier, 6 + n_y - 1)
    halos = [halo_copies(0)]
    for copy in halos[0]:
        copy.start()

    nodes = jnp.stack(
        [
            acoustic_ref[:, field, 128 * part : 128 * part + 128]
            for field in range(4)
            for part in range(4)
        ],
        0,
    )
    sound[0] = swap_groups(nodes).reshape(4, 64, 128)
    take_traces(0)
    traces = [trace_copies(0)]
    for copy in traces[0]:
        copy.start()

    widen = (iota((16, 128), 0) == eighth(iota((16, 128), 1))).astype(F32)
    owner = dot(owner_ref[...].astype(F32), widen)
    element = dot(element_ref[...].astype(F32), widen)
    rows_out = 8 * n_y
    row, column = iota((rows_out, 128), 0), iota((rows_out, 128), 1)
    same_digit = (row & 7) == (column & 7)
    earlier = (
        (eighth(iota((128, 128), 0)) < eighth(iota((128, 128), 1)))
        & ((iota((128, 128), 0) & 7) == 0)
    ).astype(F32)
    named = owner.astype(jnp.int32) == eighth(row)
    count = jnp.dot(named.astype(BF16), earlier.astype(BF16), preferred_element_type=F32)
    first, second = named & (count < 0.5), named & (count > 0.5)
    mark = jnp.where((column & 7) == 0, element + 1.0, 0.0)
    label = jnp.where(
        column < 64,
        jnp.sum(jnp.where(first, mark, 0.0), 1, keepdims=True),
        jnp.sum(jnp.where(second, mark, 0.0), 1, keepdims=True),
    )
    labels[...] = label.reshape(n_y, 8, 128)
    spread(*label_args())

    basis = basis_ref[...]
    tiled = repeat_rows(basis, 128, False)[:rows_out]
    route_ref[:, 0:128] = jnp.where(first, tiled, 0.0)
    route_ref[:, 128:256] = jnp.where(second, tiled, 0.0)
    pair_ref[...] = repeat_rows(basis, 64, True) * repeat_rows(basis, 64, False)

    derivative = derivative_ref[...]
    row64, column64 = iota((64, 64), 0), iota((64, 64), 1)
    slope_ref[0:64, :] = jnp.where(
        (row64 & 7) == (column64 & 7), repeat_rows(derivative, 64, True), 0.0
    )
    slope_ref[64:128, :] = jnp.where(
        eighth(row64) == eighth(column64), repeat_rows(derivative, 64, False), 0.0
    )
    row128, column128 = iota((128, 128), 0), iota((128, 128), 1)
    slope_z_ref[...] = jnp.where(
        eighth(row128) == eighth(column128), repeat_rows(derivative, 128, False, True), 0.0
    )

    local = (neighbour_ref[...] - place * 16).astype(F32)
    nearby = dot_tn(local, widen).astype(jnp.int32)
    row256, column256 = iota((256, 128), 0), iota((256, 128), 1)
    matching = (row256 & 7) == (column256 & 7)
    for face in range(6):
        index = nearby[face : face + 1] + (16 if face % 2 == 0 else 0)
        gather_ref[face] = (matching & (eighth(row256) == index)).astype(F32).astype(BF16)

    squared = dot(speed_ref[...], widen)
    squared = squared * squared

    def flow_stage(stage):
        for copy in halos[stage]:
            copy.wait_recv()
        fields = flow[stage].reshape(5, 8, 8, 128)
        along_x = jnp.concatenate(
            [halo_recv[stage, 0][:, None], fields, halo_recv[stage, 1][:, None]], 1
        )
        part_x = sweep(along_x, 0)
        along_y = jnp.stack(
            [halo_recv[stage, 2]]
            + [flow[stage, :, pl.ds(y, 8, stride=8), :] for y in range(8)]
            + [halo_recv[stage, 3]],
            1,
        )
        part_y = jnp.stack(sweep(along_y, 1), 0)
        for y in range(8):
            turned[:, pl.ds(y, 8, stride=8), :] = part_y[:, y]
        low, high = (
            jnp.stack(
                [
                    jnp.broadcast_to(halo_recv[stage, side][:, :, x : x + 1], (5, 8, 128))
                    for x in range(8)
                ],
                1,
            )
            for side in (4, 5)
        )
        below = jnp.where(lane == 0, low, pltpu.roll(fields, 1, 3))
        above = jnp.where(lane == 127, high, pltpu.roll(fields, 127, 3))
        part_z = [part[0] for part in sweep(jnp.stack([below, fields, above], 1), 2)]
        part_y = [turned[index].reshape(8, 8, 128) for index in range(7)]
        keep, scale = BLEND[stage]
        for index in range(5):
            rate = part_x[index] + part_y[index] + part_z[index]
            result = scale * (fields[index] + TIME_STEP * rate)
            if stage:
                result = keep * flow[0, index].reshape(8, 8, 128) + result
            if stage < 2:
                flow[stage + 1, index] = result.reshape(64, 128)
            else:
                flow_out[index] = result
        if stage < 2:
            pack_halos(stage + 1)
            halos.append(halo_copies(stage + 1))
            for copy in halos[-1]:
                copy.start()
        inverse = 1.0 / fields[0]
        speed = [fields[1 + part] * inverse for part in range(3)]
        curl = [part_y[6] - part_z[6], part_z[5] - part_x[6], part_x[5] - part_y[5]]
        lamb = [
            (curl[1] * speed[2] - curl[2] * speed[1]).reshape(64, 128),
            (curl[2] * speed[0] - curl[0] * speed[2]).reshape(64, 128),
            (curl[0] * speed[1] - curl[1] * speed[0]).reshape(64, 128),
        ]
        modes = dot(pair_ref[...], jnp.concatenate(lamb, 1))
        empty = jnp.zeros((64, 128), F32)
        doubled = []
        for part in range(3):
            piece = modes[:, 128 * part : 128 * part + 128]
            doubled.append(jnp.concatenate([piece, empty], 1))
            doubled.append(jnp.concatenate([empty, piece], 1))
        routed = dot_nt(route_ref[...], jnp.concatenate(doubled, 0))
        for part in range(3):
            packed[stage, :, part] = routed[:, 128 * part : 128 * part + 128].reshape(n_y, 8, 128)
        spread(*packet_args(stage))

    def own_rate(stage):
        state = sound[stage]
        mixed = dot(slope_ref[...], jnp.concatenate([state[0], state[1], state[2]], 1))
        depth = dot(jnp.concatenate([state[0], state[3]], 0), slope_z_ref[...])
        rate_ref[0] = -squared * (mixed[:64, 128:256] + mixed[64:, 256:] + depth[64:])
        rate_ref[1] = -mixed[:64, :128]
        rate_ref[2] = -mixed[64:, :128]
        rate_ref[3] = -depth[:64]
        for copy in traces[stage]:
            copy.wait_recv()
        jumps = []
        for face in range(6):
            axis, upper = face // 2, face % 2
            if upper:
                sides = [trace[stage, 0, axis], trace_recv[stage, 1, axis]]
            else:
                sides = [trace_recv[stage, 0, axis], trace[stage, 1, axis]]
            found = pick(
                jnp.concatenate([side.reshape(32, 128) for side in sides], 1), gather_ref[face]
            )
            jumps.append(PENALTY * (found.reshape(4, 8, 128) - trace[stage, upper, axis]))
        rate_ref[:, 0:8, :] += jumps[0]
        rate_ref[:, 56:64, :] += jumps[1]
        rate_ref[:, pl.ds(0, 8, stride=8), :] += jumps[2]
        rate_ref[:, pl.ds(7, 8, stride=8), :] += jumps[3]
        for x in range(8):
            low = pltpu.roll(jumps[4], 128 - x, 2) if x else jumps[4]
            high = pltpu.roll(jumps[5], 7 - x, 2) if x < 7 else jumps[5]
            rate_ref[:, 8 * x : 8 * x + 8, :] += jnp.where(
                digit == 0, low, jnp.where(digit == 7, high, 0.0)
            )

    def add_sources(stage):
        spread_whole(*packet_args(stage)).wait_recv()
        pieces = []
        for part in range(3):
            across = arrived[stage, :, part].reshape(rows_out, 128).T
            pieces.append(jnp.concatenate([across[:64], across[64:]], 1))
        source = pick(jnp.concatenate(pieces, 0), place_ref[...])
        keep, scale = BLEND[stage]
        results = []
        for field in range(4):
            rate = rate_ref[field]
            if field:
                rate = rate + source[64 * (field - 1) : 64 * field]
            result = scale * (sound[stage, field] + TIME_STEP * rate)
            if stage:
                result = keep * sound[0, field] + result
            results.append(result)
        return results

    flow_stage(0)

    spread_whole(*label_args()).wait_recv()
    come = labels_recv[...].reshape(rows_out, 128)
    wanted = (eighth(column) + 1).astype(F32)
    for slot in range(2):
        place_ref[slot * rows_out : (slot + 1) * rows_out, :] = (
            (same_digit & (come[:, 64 * slot : 64 * slot + 1] == wanted)).astype(F32).astype(BF16)
        )
    own_rate(0)

    flow_stage(1)
    flow_stage(2)
    for stage in range(3):
        results = add_sources(stage)
        if stage < 2:
            for field in range(4):
                sound[stage + 1, field] = results[field]
            take_traces(stage + 1)
            traces.append(trace_copies(stage + 1))
            for copy in traces[-1]:
                copy.start()
            own_rate(stage + 1)
        else:
            final = swap_groups(jnp.concatenate(results, 0).reshape(16, 16, 128))
            for field in range(4):
                for part in range(4):
                    sound_out[:, field, 128 * part : 128 * part + 128] = final[4 * field + part]

    for stage in range(3):
        for copy in halos[stage] + traces[stage]:
            copy.wait_send()
        spread_whole(*packet_args(stage)).wait_send()
    spread_whole(*label_args()).wait_send()


def solution(mesh):
    sizes = (mesh.shape["fx"], mesh.shape["fy"], mesh.shape["fz"])
    n_y = sizes[1]

    def per_device(
        density,
        velocity,
        pressure,
        acoustic,
        sound_speed,
        derivative,
        mode_basis,
        neighbours,
        block_owner,
        block_element,
    ):
        vmem = pl.BlockSpec(memory_space=pltpu.VMEM)
        return pl.pallas_call(
            functools.partial(kernel, sizes),
            out_shape=(
                jax.ShapeDtypeStruct((5, 8, 8, 128), F32),
                jax.ShapeDtypeStruct((16, 4, 512), F32),
            ),
            in_specs=[vmem] * 10,
            out_specs=(vmem, vmem),
            scratch_shapes=[
                pltpu.VMEM((3, 5, 64, 128), F32),
                pltpu.VMEM((3, 4, 5, 8, 128), F32),
                pltpu.VMEM((3, 6, 5, 8, 128), F32),
                pltpu.VMEM((7, 64, 128), F32),
                pltpu.VMEM((3, 4, 64, 128), F32),
                pltpu.VMEM((3, 2, 3, 4, 8, 128), F32),
                pltpu.VMEM((3, 2, 3, 4, 8, 128), F32),
                pltpu.VMEM((4, 64, 128), F32),
                pltpu.VMEM((3, n_y, 3, 8, 128), F32),
                pltpu.VMEM((3, n_y, 3, 8, 128), F32),
                pltpu.VMEM((n_y, 8, 128), F32),
                pltpu.VMEM((n_y, 8, 128), F32),
                pltpu.VMEM((6, 256, 128), BF16),
                pltpu.VMEM((16 * n_y, 128), BF16),
                pltpu.VMEM((8 * n_y, 256), F32),
                pltpu.VMEM((64, 64), F32),
                pltpu.VMEM((128, 64), F32),
                pltpu.VMEM((128, 128), F32),
                pltpu.SemaphoreType.DMA((3, 6)),
                pltpu.SemaphoreType.DMA((3, 6)),
                pltpu.SemaphoreType.DMA((3, 2)),
                pltpu.SemaphoreType.DMA((3, 2)),
                pltpu.SemaphoreType.DMA((3,)),
                pltpu.SemaphoreType.DMA((3,)),
                pltpu.SemaphoreType.DMA((1,)),
                pltpu.SemaphoreType.DMA((1,)),
            ],
            compiler_params=pltpu.CompilerParams(
                collective_id=0, has_side_effects=True, vmem_limit_bytes=40 * 1024 * 1024
            ),
            name="step",
        )(
            density,
            velocity,
            pressure,
            acoustic,
            sound_speed.reshape(1, 16),
            derivative,
            mode_basis,
            neighbours,
            block_owner.reshape(1, 16),
            block_element.reshape(1, 16),
        )

    placed = (
        P("fx", "fy", "fz"),
        P(None, "fx", "fy", "fz"),
        P("fx", "fy", "fz"),
        P(("fx", "fy", "fz"), None, None),
        P(("fx", "fy", "fz")),
        P(),
        P(),
        P(("fx", "fy", "fz"), None),
        P("fx", "fy", "fz", None, None),
        P("fx", "fy", "fz", None),
    )
    return jax.shard_map(
        per_device,
        mesh=mesh,
        in_specs=placed,
        out_specs=(P(None, "fx", "fy", "fz"), P(("fx", "fy", "fz"), None, None)),
        check_vma=False,
    )
```

time: 277 us -> 65.2 us (0.24)
  the two profiles are of different devices: /device:TPU:2 before, /device:TPU:6 now
where the time goes in v1:
time: 65.2 us; the launch traced here: 64.8 us
  Pallas kernels  58.1 us (89%)
  local copies, waits for them, and re-layouts  6.02 us (9%)
  between operations  0.67 us (1%)
    pallas_call x1, Pallas kernels, per_device(): pl.pallas_call(functools.partial(kernel, sizes), out_shape=(jax.ShapeDtyp...  58.1 us
    unnamed x23, local copies, waits for them, and re-layouts  6.02 us

profile of v1, /device:TPU:6, one launch (start us, length us, event | category | flops | bytes accessed | tf_op | source)
XLA Modules:
  0.0 64.8 jit_solution(5926294686210693071)
XLA Ops:
  0.6 0.0 copy-start.9
  0.6 0.7 %copy-done.9 = s32[16,6]{0,1:T(8,128)S(1)} copy-done((s32[16,6]{0,1:T(8,128)S(1)}, s32[16,6]{0,1:T(8,128)}, u32[]{:S(2)}) %copy-start.9) | copy-done | bytes 408
  1.3 0.0 copy-start.4
  1.3 0.0 copy-start.5
  1.3 0.0 copy-start.6
  1.3 0.0 copy-start.7
  1.3 0.0 copy-start.8
  1.3 0.1 copy.12.neighbour_ref
  1.4 0.6 copy-done.4
  2.0 0.0 copy-done.5
  2.0 0.0 copy-done.6
  2.0 0.0 copy-done.7
  2.0 0.0 copy-done.8
  2.0 0.0 copy-start
  2.0 0.9 %copy-done = f32[16,4,512]{2,1,0:T(4,128)S(1)} copy-done((f32[16,4,512]{2,1,0:T(4,128)S(1)}, f32[16,4,512]{2,1,0:T(4,128)}, u32[]{:S(2)}) %copy-start) | copy-done | bytes 131096
  2.9 0.0 copy-start.1
  2.9 0.9 %copy-done.1 = f32[3,8,8,128]{3,2,1,0:T(8,128)S(1)} copy-done((f32[3,8,8,128]{3,2,1,0:T(8,128)S(1)}, f32[3,8,8,128]{3,2,1,0:T(8,128)}, u32[]{:S(2)}) %copy-start.1) | copy-done | bytes 98328
  3.8 0.0 copy-start.2
  3.8 0.8 %copy-done.2 = f32[8,8,128]{2,1,0:T(8,128)S(1)} copy-done((f32[8,8,128]{2,1,0:T(8,128)S(1)}, f32[8,8,128]{2,1,0:T(8,128)}, u32[]{:S(2)}) %copy-start.2) | copy-done | bytes 32792
  4.6 0.0 copy-start.3
  4.6 0.8 %copy-done.3 = f32[8,8,128]{2,1,0:T(8,128)S(1)} copy-done((f32[8,8,128]{2,1,0:T(8,128)S(1)}, f32[8,8,128]{2,1,0:T(8,128)}, u32[]{:S(2)}) %copy-start.3) | copy-done | bytes 32792
  5.4 58.1 %step.1 = (f32[5,8,8,128]{3,2,1,0:T(8,128)S(1)}, f32[16,4,512]{2,1,0:T(4,128)S(1)}) custom-call(f32[8,8,128]{2,1,0:T(8,128)S(1)} %copy-done.2, f32[3,8,8,128]{3,2,1,0:T(8,128)S(1)} %copy-done.1, f32[8,8,128]{2,1,0:T(8,128)S(1)} %copy-done.3, f32[16,4,512]{2,1,0:T(4,128)S(1)} %copy-done, f32[1,16]{1,0:T(1,128)S(1)} %bitcast.3, f32[8,8]{1,0:T(8,128)S(1)} %copy-done.4, ...), custom_call_target="tpu_custom_call" | custom-call | tf_op jit(solution)/shard_map/step/pallas_call | solution.py:510
  63.5 0.7 %copy.15 = f32[5,8,8,128]{3,2,1,0:T(8,128)} copy(f32[5,8,8,128]{3,2,1,0:T(8,128)S(1)} %get-tuple-element.4) | data formatting | bytes 327680
  64.2 0.7 %copy.16 = f32[16,4,512]{2,1,0:T(4,128)} copy(f32[16,4,512]{2,1,0:T(4,128)S(1)} %get-tuple-element.5) | data formatting | bytes 262144
Async XLA Ops:
  0.6 0.7 %copy-start.9 = (s32[16,6]{0,1:T(8,128)S(1)}, s32[16,6]{0,1:T(8,128)}, u32[]{:S(2)}) copy-start(s32[16,6]{0,1:T(8,128)} %param.17) | copy-start | bytes 1156
  1.3 0.7 %copy-start.4 = (f32[8,8]{1,0:T(8,128)S(1)}, f32[8,8]{1,0:T(8,128)}, u32[]{:S(2)}) copy-start(f32[8,8]{1,0:T(8,128)} %derivative_ref.1) | copy-start | bytes 772
  1.3 0.7 %copy-start.5 = (f32[8,8]{1,0:T(8,128)S(1)}, f32[8,8]{1,0:T(8,128)}, u32[]{:S(2)}) copy-start(f32[8,8]{1,0:T(8,128)} %basis_ref.1) | copy-start | bytes 772
  1.3 0.7 %copy-start.6 = (f32[16]{0:T(128)S(1)}, f32[16]{0:T(128)}, u32[]{:S(2)}) copy-start(f32[16]{0:T(128)} %param.14) | copy-start | bytes 196
  1.3 0.7 %copy-start.7 = (s32[1,1,1,16,1]{3,4,2,1,0:T(1,128)S(1)}, s32[1,1,1,16,1]{3,4,2,1,0:T(1,128)}, u32[]{:S(2)}) copy-start(s32[1,1,1,16,1]{3,4,2,1,0:T(1,128)} %param.18) | copy-start | bytes 196
  1.3 0.7 %copy-start.8 = (s32[1,1,1,16]{3,2,1,0:T(1,128)S(1)}, s32[1,1,1,16]{3,2,1,0:T(1,128)}, u32[]{:S(2)}) copy-start(s32[1,1,1,16]{3,2,1,0:T(1,128)} %param.19) | copy-start | bytes 196
  2.0 0.9 %copy-start = (f32[16,4,512]{2,1,0:T(4,128)S(1)}, f32[16,4,512]{2,1,0:T(4,128)}, u32[]{:S(2)}) copy-start(f32[16,4,512]{2,1,0:T(4,128)} %acoustic_ref.1) | copy-start | bytes 393220
  2.9 0.9 %copy-start.1 = (f32[3,8,8,128]{3,2,1,0:T(8,128)S(1)}, f32[3,8,8,128]{3,2,1,0:T(8,128)}, u32[]{:S(2)}) copy-start(f32[3,8,8,128]{3,2,1,0:T(8,128)} %velocity_ref.1) | copy-start | bytes 294916
  3.8 0.8 %copy-start.2 = (f32[8,8,128]{2,1,0:T(8,128)S(1)}, f32[8,8,128]{2,1,0:T(8,128)}, u32[]{:S(2)}) copy-start(f32[8,8,128]{2,1,0:T(8,128)} %density_ref.1) | copy-start | bytes 98308
  4.6 0.8 %copy-start.3 = (f32[8,8,128]{2,1,0:T(8,128)S(1)}, f32[8,8,128]{2,1,0:T(8,128)}, u32[]{:S(2)}) copy-start(f32[8,8,128]{2,1,0:T(8,128)} %pressure_ref.1) | copy-start | bytes 98308

commit v2 on v1

--- a/solution.py
+++ b/solution.py
@@ -25,12 +25,6 @@
 def dot_nt(a, b):
     return lax.dot_general(
         a, b, (((1,), (1,)), ((), ())), precision=HIGHEST, preferred_element_type=F32
-    )
-
-
-def dot_tn(a, b):
-    return lax.dot_general(
-        a, b, (((0,), (0,)), ((), ())), precision=HIGHEST, preferred_element_type=F32
     )
 
 
@@ -100,16 +94,16 @@
 
 def kernel(
     sizes,
-    density_ref,
-    velocity_ref,
-    pressure_ref,
-    acoustic_ref,
-    speed_ref,
-    derivative_ref,
-    basis_ref,
-    neighbour_ref,
-    owner_ref,
-    element_ref,
+    density_in,
+    velocity_in,
+    pressure_in,
+    acoustic_in,
+    speed_in,
+    derivative_in,
+    basis_in,
+    neighbour_in,
+    owner_in,
+    element_in,
     flow_out,
     sound_out,
     flow,
@@ -138,6 +132,17 @@
     packed_in_sem,
     label_out_sem,
     label_in_sem,
+    density_ref,
+    velocity_ref,
+    pressure_ref,
+    acoustic_ref,
+    speed_ref,
+    derivative_ref,
+    basis_ref,
+    neighbour_ref,
+    owner_ref,
+    element_ref,
+    load_sem,
 ):
     n_x, n_y, n_z = sizes
     fx, fy, fz = lax.axis_index("fx"), lax.axis_index("fy"), lax.axis_index("fz")
@@ -165,6 +170,26 @@
         pl.semaphore_signal(
             barrier, inc=1, device_id=(fx, (fy + step) % n_y, fz), device_id_type=MESH
         )
+
+    loads = [
+        pltpu.make_async_copy(source, target, load_sem.at[index])
+        for index, (source, target) in enumerate(
+            (
+                (velocity_in, velocity_ref),
+                (density_in, density_ref),
+                (pressure_in, pressure_ref),
+                (acoustic_in, acoustic_ref),
+                (owner_in, owner_ref),
+                (element_in, element_ref),
+                (basis_in, basis_ref),
+                (derivative_in, derivative_ref),
+                (neighbour_in, neighbour_ref),
+                (speed_in, speed_ref),
+            )
+        )
+    ]
+    for copy in loads:
+        copy.start()
 
     lane = iota((8, 128), 1)
     digit = lane & 7
@@ -219,19 +244,24 @@
             for side, device in ((0, after), (1, before))
         ]
 
-    def spread(source, target, out_sem, in_sem):
-        @pl.loop(1, n_y)
-        def _(step):
-            peer = (fy + step) % n_y
-            pltpu.make_async_remote_copy(
-                src_ref=source.at[peer],
-                dst_ref=target.at[fy],
-                send_sem=out_sem,
-                recv_sem=in_sem,
-                device_id=(fx, peer, fz),
-                device_id_type=MESH,
-            ).start()
-
+    def spread(args, first=0, last=n_y):
+        source, target, out_sem, in_sem = args
+
+        @pl.loop(first, last)
+        def _(peer):
+            @pl.when(peer != fy)
+            def _():
+                pltpu.make_async_remote_copy(
+                    src_ref=source.at[peer],
+                    dst_ref=target.at[fy],
+                    send_sem=out_sem,
+                    recv_sem=in_sem,
+                    device_id=(fx, peer, fz),
+                    device_id_type=MESH,
+                ).start()
+
+    def keep_own(args):
+        source, target = args[:2]
         target[fy] = source[fy]
 
     def spread_whole(source, target, out_sem, in_sem):
@@ -255,6 +285,8 @@
             packed_in_sem.at[stage],
         )
 
+    for copy in loads[:3]:
+        copy.wait()
     density = density_ref[...].reshape(64, 128)
     speeds = velocity_ref[...].reshape(3, 64, 128)
     energy = pressure_ref[...].reshape(64, 128) / (HEAT_RATIO - 1.0) + 0.5 * density * (
@@ -271,6 +303,8 @@
     for copy in halos[0]:
         copy.start()
 
+    for copy in loads[3:]:
+        copy.wait()
     nodes = jnp.stack(
         [
             acoustic_ref[:, field, 128 * part : 128 * part + 128]
@@ -305,7 +339,8 @@
         jnp.sum(jnp.where(second, mark, 0.0), 1, keepdims=True),
     )
     labels[...] = label.reshape(n_y, 8, 128)
-    spread(*label_args())
+    spread(label_args())
+    keep_own(label_args())
 
     basis = basis_ref[...]
     tiled = repeat_rows(basis, 128, False)[:rows_out]
@@ -327,7 +362,7 @@
     )
 
     local = (neighbour_ref[...] - place * 16).astype(F32)
-    nearby = dot_tn(local, widen).astype(jnp.int32)
+    nearby = dot(local, widen).astype(jnp.int32)
     row256, column256 = iota((256, 128), 0), iota((256, 128), 1)
     matching = (row256 & 7) == (column256 & 7)
     for face in range(6):
@@ -401,7 +436,6 @@
         routed = dot_nt(route_ref[...], jnp.concatenate(doubled, 0))
         for part in range(3):
             packed[stage, :, part] = routed[:, 128 * part : 128 * part + 128].reshape(n_y, 8, 128)
-        spread(*packet_args(stage))
 
     def own_rate(stage):
         state = sound[stage]
@@ -455,6 +489,8 @@
         return results
 
     flow_stage(0)
+    spread(packet_args(0))
+    keep_own(packet_args(0))
 
     spread_whole(*label_args()).wait_recv()
     come = labels_recv[...].reshape(rows_out, 128)
@@ -466,22 +502,25 @@
     own_rate(0)
 
     flow_stage(1)
+    spread(packet_args(1))
+    keep_own(packet_args(1))
     flow_stage(2)
-    for stage in range(3):
-        results = add_sources(stage)
-        if stage < 2:
-            for field in range(4):
-                sound[stage + 1, field] = results[field]
-            take_traces(stage + 1)
-            traces.append(trace_copies(stage + 1))
-            for copy in traces[-1]:
-                copy.start()
-            own_rate(stage + 1)
-        else:
-            final = swap_groups(jnp.concatenate(results, 0).reshape(16, 16, 128))
-            for field in range(4):
-                for part in range(4):
-                    sound_out[:, field, 128 * part : 128 * part + 128] = final[4 * field + part]
+    spread(packet_args(2), 0, 5)
+    keep_own(packet_args(2))
+    for stage in range(2):
+        for field, result in enumerate(add_sources(stage)):
+            sound[stage + 1, field] = result
+        take_traces(stage + 1)
+        traces.append(trace_copies(stage + 1))
+        for copy in traces[-1]:
+            copy.start()
+        if stage == 0:
+            spread(packet_args(2), 5)
+        own_rate(stage + 1)
+    final = swap_groups(jnp.concatenate(add_sources(2), 0).reshape(16, 16, 128))
+    for field in range(4):
+        for part in range(4):
+            sound_out[:, field, 128 * part : 128 * part + 128] = final[4 * field + part]
 
     for stage in range(3):
         for copy in halos[stage] + traces[stage]:
@@ -506,14 +545,15 @@
         block_owner,
         block_element,
     ):
-        vmem = pl.BlockSpec(memory_space=pltpu.VMEM)
+        vmem, hbm = pl.BlockSpec(memory_space=pltpu.VMEM), pl.BlockSpec(memory_space=pltpu.HBM)
+        results = (
+            jax.ShapeDtypeStruct((5, 8, 8, 128), F32),
+            jax.ShapeDtypeStruct((16, 4, 512), F32),
+        )
         return pl.pallas_call(
             functools.partial(kernel, sizes),
-            out_shape=(
-                jax.ShapeDtypeStruct((5, 8, 8, 128), F32),
-                jax.ShapeDtypeStruct((16, 4, 512), F32),
-            ),
-            in_specs=[vmem] * 10,
+            out_shape=results,
+            in_specs=[hbm] * 10,
             out_specs=(vmem, vmem),
             scratch_shapes=[
                 pltpu.VMEM((3, 5, 64, 128), F32),
@@ -542,22 +582,38 @@
                 pltpu.SemaphoreType.DMA((3,)),
                 pltpu.SemaphoreType.DMA((1,)),
                 pltpu.SemaphoreType.DMA((1,)),
+                pltpu.VMEM((8, 8, 128), F32),
+                pltpu.VMEM((3, 8, 8, 128), F32),
+                pltpu.VMEM((8, 8, 128), F32),
+                pltpu.VMEM((16, 4, 512), F32),
+                pltpu.VMEM((1, 16), F32),
+                pltpu.VMEM((8, 8), F32),
+                pltpu.VMEM((8, 8), F32),
+                pltpu.VMEM((6, 16), jnp.int32),
+                pltpu.VMEM((1, 16), jnp.int32),
+                pltpu.VMEM((1, 16), jnp.int32),
+                pltpu.SemaphoreType.DMA((10,)),
             ],
             compiler_params=pltpu.CompilerParams(
                 collective_id=0, has_side_effects=True, vmem_limit_bytes=40 * 1024 * 1024
             ),
             name="step",
         )(
-            density,
-            velocity,
-            pressure,
-            acoustic,
-            sound_speed.reshape(1, 16),
-            derivative,
-            mode_basis,
-            neighbours,
-            block_owner.reshape(1, 16),
-            block_element.reshape(1, 16),
+            *(
+                pltpu.with_memory_space_constraint(value, pltpu.HBM)
+                for value in (
+                    density,
+                    velocity,
+                    pressure,
+                    acoustic,
+                    sound_speed.reshape(1, 16),
+                    derivative,
+                    mode_basis,
+                    neighbours.T,
+                    block_owner.reshape(1, 16),
+                    block_element.reshape(1, 16),
+                )
+            )
         )
 
     placed = (

time: 65.2 us -> 58.1 us (0.89)
  the two profiles are of different devices: /device:TPU:6 before, /device:TPU:1 now
where the time goes in v2:
time: 58.1 us; the launch traced here: 58 us
  Pallas kernels  56 us (96%)
  local copies, waits for them, and re-layouts  1.32 us (2%)
  between operations  0.64 us (1%)
    pallas_call x1, Pallas kernels, per_device(): pl.pallas_call(functools.partial(kernel, sizes), out_shape=results, in_sp...  56 us
    unnamed x2, local copies, waits for them, and re-layouts  1.32 us

profile of v2, /device:TPU:1, one launch (start us, length us, event | category | flops | bytes accessed | tf_op | source)
XLA Modules:
  0.0 58.0 jit_solution(16464582869912976655)
XLA Ops:
  0.6 56.0 %step.1 = (f32[5,8,8,128]{3,2,1,0:T(8,128)S(1)}, f32[16,4,512]{2,1,0:T(4,128)S(1)}) custom-call(f32[8,8,128]{2,1,0:T(8,128)} %density_in.1, f32[3,8,8,128]{3,2,1,0:T(8,128)} %velocity_in.1, f32[8,8,128]{2,1,0:T(8,128)} %pressure_in.1, f32[16,4,512]{2,1,0:T(4,128)} %acoustic_in.1, f32[1,16]{1,0:T(1,128)} %bitcast.5, f32[8,8]{1,0:T(8,128)} %derivative_in.1, ...), custom_call_target="tpu_custom_call" | custom-call | tf_op jit(solution)/shard_map/step/pallas_call | solution.py:553
  56.7 0.7 %copy.14 = f32[5,8,8,128]{3,2,1,0:T(8,128)} copy(f32[5,8,8,128]{3,2,1,0:T(8,128)S(1)} %get-tuple-element.4) | data formatting | bytes 327680
  57.3 0.7 %copy.15 = f32[16,4,512]{2,1,0:T(4,128)} copy(f32[16,4,512]{2,1,0:T(4,128)S(1)} %get-tuple-element.5) | data formatting | bytes 262144

commit v3 on v2

--- a/solution.py
+++ b/solution.py
@@ -248,7 +248,9 @@
         source, target, out_sem, in_sem = args
 
         @pl.loop(first, last)
-        def _(peer):
+        def _(rank):
+            peer = (rank + n_y - 1) % n_y
+
             @pl.when(peer != fy)
             def _():
                 pltpu.make_async_remote_copy(
@@ -488,6 +490,14 @@
             results.append(result)
         return results
 
+    def next_sound(stage):
+        for field, result in enumerate(add_sources(stage)):
+            sound[stage + 1, field] = result
+        take_traces(stage + 1)
+        traces.append(trace_copies(stage + 1))
+        for copy in traces[-1]:
+            copy.start()
+
     flow_stage(0)
     spread(packet_args(0))
     keep_own(packet_args(0))
@@ -504,19 +514,14 @@
     flow_stage(1)
     spread(packet_args(1))
     keep_own(packet_args(1))
+    next_sound(0)
     flow_stage(2)
-    spread(packet_args(2), 0, 5)
+    spread(packet_args(2), 0, 6)
     keep_own(packet_args(2))
-    for stage in range(2):
-        for field, result in enumerate(add_sources(stage)):
-            sound[stage + 1, field] = result
-        take_traces(stage + 1)
-        traces.append(trace_copies(stage + 1))
-        for copy in traces[-1]:
-            copy.start()
-        if stage == 0:
-            spread(packet_args(2), 5)
-        own_rate(stage + 1)
+    own_rate(1)
+    spread(packet_args(2), 6)
+    next_sound(1)
+    own_rate(2)
     final = swap_groups(jnp.concatenate(add_sources(2), 0).reshape(16, 16, 128))
     for field in range(4):
         for part in range(4):
@@ -527,6 +532,17 @@
             copy.wait_send()
         spread_whole(*packet_args(stage)).wait_send()
     spread_whole(*label_args()).wait_send()
+
+
+def hand_over(flow_in, sound_in, flow_result, sound_result, sem):
+    copies = [
+        pltpu.make_async_copy(flow_in, flow_result, sem.at[0]),
+        pltpu.make_async_copy(sound_in, sound_result, sem.at[1]),
+    ]
+    for copy in copies:
+        copy.start()
+    for copy in copies:
+        copy.wait()
 
 
 def solution(mesh):
@@ -550,7 +566,7 @@
             jax.ShapeDtypeStruct((5, 8, 8, 128), F32),
             jax.ShapeDtypeStruct((16, 4, 512), F32),
         )
-        return pl.pallas_call(
+        states = pl.pallas_call(
             functools.partial(kernel, sizes),
             out_shape=results,
             in_specs=[hbm] * 10,
@@ -615,6 +631,15 @@
                 )
             )
         )
+        return pl.pallas_call(
+            hand_over,
+            out_shape=results,
+            in_specs=[vmem, vmem],
+            out_specs=(hbm, hbm),
+            scratch_shapes=[pltpu.SemaphoreType.DMA((2,))],
+            compiler_params=pltpu.CompilerParams(vmem_limit_bytes=40 * 1024 * 1024),
+            name="hand_over",
+        )(*states)
 
     placed = (
         P("fx", "fy", "fz"),

time: 58.1 us -> 54.4 us (0.936)
  the two profiles are of different devices: /device:TPU:1 before, /device:TPU:2 now
where the time goes in v3:
time: 54.4 us; the launch traced here: 54.2 us
  Pallas kernels  53.6 us (99%)
  between operations  0.64 us (1%)
    pallas_call x1, Pallas kernels, per_device(): pl.pallas_call(functools.partial(kernel, sizes), out_shape=results, in_sp...  52.9 us

profile of v3, /device:TPU:2, one launch (start us, length us, event | category | flops | bytes accessed | tf_op | source)
XLA Modules:
  0.0 54.2 jit_solution(10952812333594953218)
XLA Ops:
  0.6 52.9 %step.1 = (f32[5,8,8,128]{3,2,1,0:T(8,128)S(1)}, f32[16,4,512]{2,1,0:T(4,128)S(1)}) custom-call(f32[8,8,128]{2,1,0:T(8,128)} %density_in.1, f32[3,8,8,128]{3,2,1,0:T(8,128)} %velocity_in.1, f32[8,8,128]{2,1,0:T(8,128)} %pressure_in.1, f32[16,4,512]{2,1,0:T(4,128)} %acoustic_in.1, f32[1,16]{1,0:T(1,128)} %bitcast.5, f32[8,8]{1,0:T(8,128)} %derivative_in.1, ...), custom_call_target="tpu_custom_call" | custom-call | tf_op jit(solution)/shard_map/step/pallas_call | solution.py:569
  53.5 0.7 %hand_over.1 = (f32[5,8,8,128]{3,2,1,0:T(8,128)}, f32[16,4,512]{2,1,0:T(4,128)}) custom-call(f32[5,8,8,128]{3,2,1,0:T(8,128)S(1)} %get-tuple-element.4.flow_in, f32[16,4,512]{2,1,0:T(4,128)S(1)} %get-tuple-element.5.sound_in), custom_call_target="tpu_custom_call" | custom-call | tf_op jit(solution)/shard_map/hand_over/pallas_call | solution.py:634

commit v4 on v3

--- a/solution.py
+++ b/solution.py
@@ -511,10 +511,23 @@
         )
     own_rate(0)
 
+    crossing = (fz == 0) | (fz == n_z - 1)
+    inner = (fz != 0) & (fz != n_z - 1)
     flow_stage(1)
-    spread(packet_args(1))
+
+    spread(packet_args(1), 0, 3)
+
+    @pl.when(crossing)
+    def _():
+        spread(packet_args(1), 3)
+
     keep_own(packet_args(1))
     next_sound(0)
+
+    @pl.when(inner)
+    def _():
+        spread(packet_args(1), 3)
+
     flow_stage(2)
     spread(packet_args(2), 0, 6)
     keep_own(packet_args(2))

time: 54.4 us -> 54.4 us (level)
  no operation moved by 1% of the time
where the time goes in v4:
time: 54.4 us; the launch traced here: 54.2 us
  Pallas kernels  53.6 us (99%)
  between operations  0.64 us (1%)
    pallas_call x1, Pallas kernels, per_device(): pl.pallas_call(functools.partial(kernel, sizes), out_shape=results, in_sp...  52.9 us

profile of v4, /device:TPU:2, one launch (start us, length us, event | category | flops | bytes accessed | tf_op | source)
XLA Modules:
  0.0 54.2 jit_solution(2891659308583637621)
XLA Ops:
  0.6 52.9 %step.1 = (f32[5,8,8,128]{3,2,1,0:T(8,128)S(1)}, f32[16,4,512]{2,1,0:T(4,128)S(1)}) custom-call(f32[8,8,128]{2,1,0:T(8,128)} %density_in.1, f32[3,8,8,128]{3,2,1,0:T(8,128)} %velocity_in.1, f32[8,8,128]{2,1,0:T(8,128)} %pressure_in.1, f32[16,4,512]{2,1,0:T(4,128)} %acoustic_in.1, f32[1,16]{1,0:T(1,128)} %bitcast.5, f32[8,8]{1,0:T(8,128)} %derivative_in.1, ...), custom_call_target="tpu_custom_call" | custom-call | tf_op jit(solution)/shard_map/step/pallas_call | solution.py:582
  53.5 0.7 %hand_over.1 = (f32[5,8,8,128]{3,2,1,0:T(8,128)}, f32[16,4,512]{2,1,0:T(4,128)}) custom-call(f32[5,8,8,128]{3,2,1,0:T(8,128)S(1)} %get-tuple-element.4.flow_in, f32[16,4,512]{2,1,0:T(4,128)S(1)} %get-tuple-element.5.sound_in), custom_call_target="tpu_custom_call" | custom-call | tf_op jit(solution)/shard_map/hand_over/pallas_call | solution.py:647

commit v5 on v4

--- a/solution.py
+++ b/solution.py
@@ -161,16 +161,6 @@
         (fx, fy, (fz + 1) % n_z),
         (fx, fy, (fz + n_z - 1) % n_z),
     ]
-    barrier = pltpu.get_barrier_semaphore()
-    for device in [beside[0], beside[1], beside[4], beside[5], after, before]:
-        pl.semaphore_signal(barrier, inc=1, device_id=device, device_id_type=MESH)
-
-    @pl.loop(1, n_y)
-    def _(step):
-        pl.semaphore_signal(
-            barrier, inc=1, device_id=(fx, (fy + step) % n_y, fz), device_id_type=MESH
-        )
-
     loads = [
         pltpu.make_async_copy(source, target, load_sem.at[index])
         for index, (source, target) in enumerate(
@@ -190,6 +180,16 @@
     ]
     for copy in loads:
         copy.start()
+
+    barrier = pltpu.get_barrier_semaphore()
+    for device in [beside[0], beside[1], beside[4], beside[5], after, before]:
+        pl.semaphore_signal(barrier, inc=1, device_id=device, device_id_type=MESH)
+
+    @pl.loop(1, n_y)
+    def _(step):
+        pl.semaphore_signal(
+            barrier, inc=1, device_id=(fx, (fy + step) % n_y, fz), device_id_type=MESH
+        )
 
     lane = iota((8, 128), 1)
     digit = lane & 7

time: 54.4 us -> 54.4 us (level)
  no operation moved by 1% of the time
where the time goes in v5:
time: 54.4 us; the launch traced here: 54.3 us
  Pallas kernels  53.6 us (99%)
  between operations  0.64 us (1%)
    pallas_call x1, Pallas kernels, per_device(): pl.pallas_call(functools.partial(kernel, sizes), out_shape=results, in_sp...  52.9 us

profile of v5, /device:TPU:2, one launch (start us, length us, event | category | flops | bytes accessed | tf_op | source)
XLA Modules:
  0.0 54.3 jit_solution(11071847127089831452)
XLA Ops:
  0.6 52.9 %step.1 = (f32[5,8,8,128]{3,2,1,0:T(8,128)S(1)}, f32[16,4,512]{2,1,0:T(4,128)S(1)}) custom-call(f32[8,8,128]{2,1,0:T(8,128)} %density_in.1, f32[3,8,8,128]{3,2,1,0:T(8,128)} %velocity_in.1, f32[8,8,128]{2,1,0:T(8,128)} %pressure_in.1, f32[16,4,512]{2,1,0:T(4,128)} %acoustic_in.1, f32[1,16]{1,0:T(1,128)} %bitcast.5, f32[8,8]{1,0:T(8,128)} %derivative_in.1, ...), custom_call_target="tpu_custom_call" | custom-call | tf_op jit(solution)/shard_map/step/pallas_call | solution.py:582
  53.5 0.7 %hand_over.1 = (f32[5,8,8,128]{3,2,1,0:T(8,128)}, f32[16,4,512]{2,1,0:T(4,128)}) custom-call(f32[5,8,8,128]{3,2,1,0:T(8,128)S(1)} %get-tuple-element.4.flow_in, f32[16,4,512]{2,1,0:T(4,128)S(1)} %get-tuple-element.5.sound_in), custom_call_target="tpu_custom_call" | custom-call | tf_op jit(solution)/shard_map/hand_over/pallas_call | solution.py:647
